TPU v7x, 32 devices: a whole 2x2x4 slice. The times are simulated.
32 devices in a mesh: ctxlo: 4 (over z), ctxhi: 8 (over y, x, core).
Axes of the slice: x: 2, y: 2, z: 4, core: 2. Of those that a mesh axis runs over, the one named last changes fastest.
Arguments:
- query_matrix: float32 [8192, 1536], P(('ctxhi', 'ctxlo')), may hold values from -6 to 6
- key_matrix: float32 [8192, 256], P(('ctxhi', 'ctxlo')), may hold values from -6 to 6
- value_matrix: float32 [8192, 256], P(('ctxhi', 'ctxlo')), may hold values from -24 to 24
- block_lists: int32 [64, 15], P(('ctxhi', 'ctxlo')), may hold values from -1 to 63, as said below
Outputs:
- attended: float32 [8192, 1536], P(('ctxhi', 'ctxlo'))
Inputs may be any that keep to these rules, and one draw needn't show every extreme that they name: `block_lists`: row q holds distinct key blocks, each one of q, q - 1, q - 2, q - 3 and q - 2**j for j >= 2, never below 0, always including q itself, in any order; the other slots hold -1.
All inputs are finite; a program needn't handle non-finite values.
Results may differ from a plain program's by a relative error of at most 0.0003.
Values sent between devices are 32-bit elements; how exact they have to be, the bound alone decides.
No kernel may reach another device: no remote copies, remote signals or barrier semaphores. Data moves between devices by JAX's collectives and lax.ppermute only.
A program may use at most 64 MiB of HBM per device.

v0:
```python
import jax
import jax.numpy as jnp
from jax import lax
from jax.sharding import PartitionSpec as P

QUERY_HEADS = 12
KEY_VALUE_HEADS = 2
HEAD_FEATURES = 128
BLOCK_TOKENS = 128


def shifted(block, axis, distance):
    devices = range(lax.axis_size(axis))
    route = [((i - distance) % len(devices), i) for i in devices]
    return lax.ppermute(block, axis, route)


def shifted_2(block, axis, distance):
    devices = range(lax.axis_size(axis))
    route = [(i - distance, i) for i in devices if i - distance in devices]
    return lax.ppermute(block, axis, route)


def body(query_matrix, key_matrix, value_matrix, block_lists):
    per_device = query_matrix.shape[0] // BLOCK_TOKENS
    inner_size = lax.axis_size("ctxlo")
    outer_size = lax.axis_size("ctxhi")
    inner_index = lax.axis_index("ctxlo")
    outer_index = lax.axis_index("ctxhi")
    device_index = outer_index * inner_size + inner_index
    block_count = per_device * inner_size * outer_size
    distances = [0, 1, 2, 3] + [
        2**power_level for power_level in range(2, 40) if 2**power_level < block_count
    ]
    key_value = jnp.concatenate([key_matrix, value_matrix], axis=1)
    needed = sorted(
        {
            -((local_block - distance) // per_device)
            for distance in distances
            for local_block in range(per_device)
        }
        - {0}
    )
    shards = {0: key_value}
    for offset in needed:
        inner_step = offset % inner_size
        outer_hop = offset // inner_size
        inner_moved = shifted(key_value, "ctxlo", inner_step) if inner_step else key_value
        direct = shifted_2(inner_moved, "ctxhi", outer_hop) if outer_hop else inner_moved
        if inner_step:
            if outer_hop + 1 < outer_size:
                carried = shifted_2(inner_moved, "ctxhi", outer_hop + 1)
            else:
                carried = jnp.zeros_like(inner_moved)
            shards[offset] = jnp.where(inner_index >= inner_step, direct, carried)
        else:
            shards[offset] = direct
    group_width = QUERY_HEADS // KEY_VALUE_HEADS
    score_scale = HEAD_FEATURES ** (-0.5)
    distance_array = jnp.array(distances, jnp.int32)
    row_ids = lax.broadcasted_iota(jnp.int32, (BLOCK_TOKENS, 1, BLOCK_TOKENS), 0)
    col_ids = lax.broadcasted_iota(jnp.int32, (BLOCK_TOKENS, 1, BLOCK_TOKENS), 2)
    causal = col_ids <= row_ids
    outputs = []
    for local_block in range(per_device):
        query_block_index = device_index * per_device + local_block
        pieces = []
        for distance in distances:
            offset = -((local_block - distance) // per_device)
            row_start = (local_block - distance) % per_device * BLOCK_TOKENS
            pieces.append(shards[offset][row_start : row_start + BLOCK_TOKENS])
        collected_rows = jnp.concatenate(pieces, axis=0)
        targets = query_block_index - distance_array
        listed = jnp.any(block_lists[local_block][None, :] == targets[:, None], axis=1) & (
            targets >= 0
        )
        allowed = listed[None, :, None] & ((distance_array[None, :, None] > 0) | causal)
        allowed = allowed.reshape(BLOCK_TOKENS, len(distances) * BLOCK_TOKENS)
        query_block_rows = query_matrix[
            local_block * BLOCK_TOKENS : (local_block + 1) * BLOCK_TOKENS
        ]
        head_outputs = []
        for head_cluster in range(KEY_VALUE_HEADS):
            query_portion = query_block_rows[
                :,
                head_cluster
                * group_width
                * HEAD_FEATURES : (head_cluster + 1)
                * group_width
                * HEAD_FEATURES,
            ].reshape(BLOCK_TOKENS, group_width, HEAD_FEATURES)
            key_portion = collected_rows[
                :, head_cluster * HEAD_FEATURES : (head_cluster + 1) * HEAD_FEATURES
            ]
            value_portion = collected_rows[
                :,
                (KEY_VALUE_HEADS + head_cluster)
                * HEAD_FEATURES : (KEY_VALUE_HEADS + head_cluster + 1)
                * HEAD_FEATURES,
            ]
            scores = (
                jnp.einsum(
                    "rgd,kd->grk", query_portion, key_portion, precision=lax.Precision.HIGHEST
                )
                * score_scale
            )
            scores = jnp.where(allowed[None], scores, -jnp.inf)
            row_max = jnp.max(scores, axis=2, keepdims=True)
            weights = jnp.exp(scores - row_max)
            denominator = jnp.sum(weights, axis=2)
            weighted = jnp.einsum(
                "grk,kd->rgd", weights, value_portion, precision=lax.Precision.HIGHEST
            )
            head_outputs.append(
                (weighted / jnp.transpose(denominator)[:, :, None]).reshape(
                    BLOCK_TOKENS, group_width * HEAD_FEATURES
                )
            )
        outputs.append(jnp.concatenate(head_outputs, axis=1))
    return jnp.concatenate(outputs, axis=0)


def solution(mesh):
    in_specs = (
        P(("ctxhi", "ctxlo"), None),
        P(("ctxhi", "ctxlo"), None),
        P(("ctxhi", "ctxlo"), None),
        P(("ctxhi", "ctxlo"), None),
    )
    out_specs = P(("ctxhi", "ctxlo"), None)
    return jax.shard_map(body, mesh=mesh, in_specs=in_specs, out_specs=out_specs, check_vma=False)
```

profile of v0, /device:TPU:4, one launch (start us, length us, event | category | flops | bytes accessed | tf_op | source)
XLA Modules:
  0.0 97.8 jit_solution(969089838487201159)
XLA Ops:
  2.0 1.6 %collective-permute-start = (f32[256,512]{1,0:T(8,128)S(1)}, f32[256,512]{1,0:T(8,128)}, u32[]{:S(2)}, u32[]{:S(2)}) collective-permute-start(f32[256,512]{1,0:T(8,128)S(1)} %constant_dynamic-update-slice_fusion), channel_id=1, source_target_pairs={{24,0},{0,8},{8,16},{16,24},{25,1},{1,9},{9,17},{17,25},{26,2},{2,... | collective-permute-start | bytes 1572872 | tf_op jit(solution)/shard_map/ppermute | solution.py:15
  3.6 2.6 %collective-permute-start.2 = (f32[256,512]{1,0:T(8,128)S(1)}, f32[256,512]{1,0:T(8,128)}, u32[]{:S(2)}, u32[]{:S(2)}) collective-permute-start(f32[256,512]{1,0:T(8,128)S(1)} %constant_dynamic-update-slice_fusion), channel_id=1, source_target_pairs={{16,0},{24,8},{0,16},{8,24},{17,1},{25,9},{1,17},{9,25},{18,2},{26... | collective-permute-start | bytes 1572872 | tf_op jit(solution)/shard_map/ppermute | solution.py:15
  6.2 1.9 %collective-permute-start.4 = (f32[256,512]{1,0:T(8,128)S(1)}, f32[256,512]{1,0:T(8,128)}, u32[]{:S(2)}, u32[]{:S(2)}) collective-permute-start(f32[256,512]{1,0:T(8,128)S(1)} %constant_dynamic-update-slice_fusion), channel_id=1, source_target_pairs={{0,1},{1,2},{2,3},{3,4},{4,5},{5,6},{6,7},{8,9},{9,10},{10,11},{11... | collective-permute-start | bytes 1572872 | tf_op jit(solution)/shard_map/ppermute | solution.py:21
  8.1 3.4 %collective-permute-start.5 = (f32[256,512]{1,0:T(8,128)S(1)}, f32[256,512]{1,0:T(8,128)S(1)}, u32[]{:S(2)}, u32[]{:S(2)}) collective-permute-start(f32[256,512]{1,0:T(8,128)S(1)} %constant_dynamic-update-slice_fusion), channel_id=1, source_target_pairs={{0,2},{1,3},{2,4},{3,5},{4,6},{5,7},{8,10},{9,11},{10,12},{11,13},... | collective-permute-start | bytes 1572872 | tf_op jit(solution)/shard_map/ppermute | solution.py:21
  17.7 1.5 %fusion.50 = (f32[128,768]{1,0:T(8,128)S(1)}, f32[128,768]{1,0:T(8,128)S(1)}, f32[128,768]{1,0:T(8,128)S(1)}, f32[128,768]{1,0:T(8,128)S(1)}) fusion(f32[256,1536]{1,0:T(8,128)} %param.5), kind=kLoop, calls=%fused_computation.100 | loop fusion | bytes 3145728 | tf_op jit(solution)/shard_map/slice | solution.py:84
  19.2 2.0 %collective-permute-start.1 = (f32[256,512]{1,0:T(8,128)}, f32[256,512]{1,0:T(8,128)}, u32[]{:S(2)}, u32[]{:S(2)}) collective-permute-start(f32[256,512]{1,0:T(8,128)} %collective-permute-done), channel_id=1, source_target_pairs={{0,1},{1,2},{2,3},{3,4},{4,5},{5,6},{6,7},{8,9},{9,10},{10,11},{11... | collective-permute-start | bytes 1572872 | tf_op jit(solution)/shard_map/ppermute | solution.py:21
  23.4 2.0 %fusion.41 = (pred[128,1024]{0,1:T(8,128)(4,1)S(1)}, pred[128,1024]{0,1:T(8,128)(4,1)}) fusion(pred[1024]{0:T(1024)(128)(4,1)} %broadcast_bitcast_fusion, pred[1024]{0:T(1024)(128)(4,1)} %broadcast_bitcast_fusion.2, pred[128,128]{0,1:T(8,128)(4,1)S(1)} %iota_compare_fusion, pred[1024]{0:T(1024)(128)(4,1)} %broadcast_bitcast_fusion.1), kind=kLoop, calls=%fused_computation.59 | loop fusion | flops 393216 | bytes 281600 | tf_op jit(solution)/shard_map/and | solution.py:77
  25.5 14.6 %collective-permute-done.2 = f32[256,512]{1,0:T(8,128)} collective-permute-done((f32[256,512]{1,0:T(8,128)S(1)}, f32[256,512]{1,0:T(8,128)}, u32[]{:S(2)}, u32[]{:S(2)}) %collective-permute-start.2) | collective-permute-done | bytes 524320 | tf_op jit(solution)/shard_map/ppermute | solution.py:15
  40.1 1.9 %collective-permute-start.3 = (f32[256,512]{1,0:T(8,128)}, f32[256,512]{1,0:T(8,128)S(1)}, u32[]{:S(2)}, u32[]{:S(2)}) collective-permute-start(f32[256,512]{1,0:T(8,128)} %collective-permute-done.2), channel_id=1, source_target_pairs={{0,1},{1,2},{2,3},{3,4},{4,5},{5,6},{6,7},{8,9},{9,10},{10,11},{11... | collective-permute-start | bytes 1572872 | tf_op jit(solution)/shard_map/ppermute | solution.py:21
  43.3 8.5 %collective-permute-done.3 = f32[256,512]{1,0:T(8,128)S(1)} collective-permute-done((f32[256,512]{1,0:T(8,128)}, f32[256,512]{1,0:T(8,128)S(1)}, u32[]{:S(2)}, u32[]{:S(2)}) %collective-permute-start.3) | collective-permute-done | bytes 524320 | tf_op jit(solution)/shard_map/ppermute | solution.py:21
  53.1 1.3 %copy-done.6 = f32[1024,512]{1,0:T(8,128)} copy-done((f32[1024,512]{1,0:T(8,128)}, f32[1024,512]{1,0:T(8,128)S(1)}, u32[]{:S(2)}) %copy-start.6) | copy-done | bytes 2097176
  54.5 3.0 %fusion.8 = (f32[6,128]{1,0:T(8,128)S(1)}, f32[1024,128,6]{1,0,2:T(8,128)S(1)}) fusion(pred[128,1024]{0,1:T(8,128)(4,1)S(1)} %get-tuple-element.25, f32[128,6,128]{0,2,1:T(8,128)S(1)} %bitcast.133, f32[1024,512]{1,0:T(8,128)S(1)} %get-tuple-element.13), kind=kOutput, calls=%fused_computation.16 | convolution fusion | flops 1210318080 | bytes 4197376 | tf_op jit(solution)/shard_map/rgd,kd->grk/dot_general | solution.py:102
  57.4 3.4 %fusion = (f32[6,128]{1,0:T(8,128)S(1)}, f32[6,128]{1,0:T(8,128)S(1)}, f32[1024,128,6]{1,0,2:T(8,128)S(1)}) fusion(f32[1024,128,6]{1,0,2:T(8,128)S(1)} %get-tuple-element.37, f32[6,128]{1,0:T(8,128)S(1)} %get-tuple-element.36, pred[128,1024]{0,1:T(8,128)(4,1)S(1)} %get-tuple-element.25, f32[128,6,128]{0,2,1:T(8,128)S(1)} %bitcast.135, ...), kind=kOutput, calls=%fused_computation.8 | convolution fusion | flops 1213463040 | bytes 7350272 | tf_op jit(solution)/shard_map/rgd,kd->grk/dot_general | solution.py:102
  60.9 3.4 %fusion.32 = f32[128,6,128]{0,2,1:T(8,128)} fusion(f32[1024,128,6]{1,0,2:T(8,128)S(1)} %get-tuple-element.37, f32[6,128]{1,0:T(8,128)S(1)} %get-tuple-element.36, pred[128,1024]{0,1:T(8,128)(4,1)S(1)} %get-tuple-element.25, f32[1024,512]{1,0:T(8,128)S(1)} %get-tuple-element.13, f32[128,6]{0,1:T(8,128)S(1)} %bitcast.142), kind=kOutput, calls=%fused_computation.41 | convolution fusion | flops 1210417152 | bytes 4202496 | tf_op jit(solution)/shard_map/grk,kd->rgd/dot_general | solution.py:111
  64.3 1.9 %copy.46 = f32[128,768]{1,0:T(8,128)} copy(f32[128,768]{0,1:T(8,128)} %bitcast.138) | data formatting | bytes 786432 | tf_op jit(solution)/shard_map/reshape | solution.py:115
  66.2 1.6 %fusion.2 = f32[6,128]{1,0:T(8,128)S(1)} fusion(f32[1024,128,6]{1,0,2:T(8,128)S(1)} %get-tuple-element.38, f32[6,128]{1,0:T(8,128)S(1)} %get-tuple-element.6, pred[128,1024]{0,1:T(8,128)(4,1)} %copy-done.2), kind=kLoop, calls=%fused_computation.10 | loop fusion | flops 3144960 | bytes 3282944 | tf_op jit(solution)/shard_map/reduce_sum | solution.py:110
  67.8 4.5 %fusion.33 = f32[128,6,128]{0,2,1:T(8,128)} fusion(f32[1024,128,6]{1,0,2:T(8,128)S(1)} %get-tuple-element.38, f32[6,128]{1,0:T(8,128)S(1)} %get-tuple-element.6, pred[128,1024]{0,1:T(8,128)(4,1)S(1)} %copy-done.3, f32[1024,512]{1,0:T(8,128)} %copy-done.5, f32[128,6]{0,1:T(8,128)S(1)} %bitcast.140), kind=kOutput, calls=%fused_computation.42 | convolution fusion | flops 1210417152 | bytes 4200448 | tf_op jit(solution)/shard_map/grk,kd->rgd/dot_general | solution.py:111
  72.3 2.0 %copy.47 = f32[128,768]{1,0:T(8,128)} copy(f32[128,768]{0,1:T(8,128)} %bitcast.136) | data formatting | bytes 786432 | tf_op jit(solution)/shard_map/reshape | solution.py:115
  74.3 4.0 %fusion.10 = (f32[6,128]{1,0:T(8,128)S(1)}, f32[1024,128,6]{1,0,2:T(8,128)S(1)}) fusion(pred[128,1024]{0,1:T(8,128)(4,1)} %get-tuple-element.26, f32[128,6,128]{0,2,1:T(8,128)S(1)} %bitcast.132, f32[1024,512]{1,0:T(8,128)} %copy-done.6), kind=kOutput, calls=%fused_computation.18 | convolution fusion | flops 1210318080 | bytes 4197376 | tf_op jit(solution)/shard_map/rgd,kd->grk/dot_general | solution.py:102
  78.3 4.6 %fusion.4 = (f32[6,128]{1,0:T(8,128)S(1)}, f32[6,128]{1,0:T(8,128)S(1)}, f32[1024,128,6]{1,0,2:T(8,128)S(1)}) fusion(f32[1024,128,6]{1,0,2:T(8,128)S(1)} %get-tuple-element.34, f32[6,128]{1,0:T(8,128)S(1)} %get-tuple-element.33, pred[128,1024]{0,1:T(8,128)(4,1)S(1)} %copy-done.1, f32[128,6,128]{0,2,1:T(8,128)} %bitcast.134, f32[1024,512]{1,0:T(8,128)} %copy-done.6), kind=kOutput, calls=%fused_computation.12 | convolution fusion | flops 1213463040 | bytes 7349248 | tf_op jit(solution)/shard_map/rgd,kd->grk/dot_general | solution.py:102
  82.9 4.3 %fusion.34 = f32[128,6,128]{0,2,1:T(8,128)} fusion(f32[1024,128,6]{1,0,2:T(8,128)S(1)} %get-tuple-element.34, f32[6,128]{1,0:T(8,128)S(1)} %get-tuple-element.33, pred[128,1024]{0,1:T(8,128)(4,1)S(1)} %copy-done.1, f32[1024,512]{1,0:T(8,128)} %copy-done.6, f32[128,6]{0,1:T(8,128)S(1)} %bitcast.143), kind=kOutput, calls=%fused_computation.43 | convolution fusion | flops 1210417152 | bytes 4200448 | tf_op jit(solution)/shard_map/grk,kd->rgd/dot_general | solution.py:111
  87.2 1.9 %copy.56 = f32[128,768]{1,0:T(8,128)} copy(f32[128,768]{0,1:T(8,128)} %bitcast.139) | data formatting | bytes 786432 | tf_op jit(solution)/shard_map/reshape | solution.py:115
  89.8 4.4 %fusion.35 = f32[128,6,128]{0,2,1:T(8,128)} fusion(f32[1024,128,6]{1,0,2:T(8,128)S(1)} %get-tuple-element.35, f32[6,128]{1,0:T(8,128)S(1)} %get-tuple-element.8, pred[128,1024]{0,1:T(8,128)(4,1)} %get-tuple-element.26, f32[1024,512]{1,0:T(8,128)} %copy-done.6, f32[128,6]{0,1:T(8,128)S(1)} %bitcast.141), kind=kOutput, calls=%fused_computation.44 | convolution fusion | flops 1210417152 | bytes 4200448 | tf_op jit(solution)/shard_map/grk,kd->rgd/dot_general | solution.py:111
  95.4 2.4 %maximum_maximum_fusion = f32[256,1536]{1,0:T(8,128)} fusion(f32[128,768]{1,0:T(8,128)S(1)} %copy.57, f32[128,768]{1,0:T(8,128)} %copy.56, f32[128,768]{1,0:T(8,128)} %copy.47, f32[128,768]{1,0:T(8,128)S(1)} %copy-done), kind=kLoop, calls=%fused_computation.20 | loop fusion | flops 1179648 | bytes 3145728 | tf_op jit(solution)/shard_map/concatenate | solution.py:120
  (47 shorter events, 14.7 us)
Async XLA Ops:
  2.0 17.2 %collective-permute-start = (f32[256,512]{1,0:T(8,128)S(1)}, f32[256,512]{1,0:T(8,128)}, u32[]{:S(2)}, u32[]{:S(2)}) collective-permute-start(f32[256,512]{1,0:T(8,128)S(1)} %constant_dynamic-update-slice_fusion), channel_id=1, source_target_pairs={{24,0},{0,8},{8,16},{16,24},{25,1},{1,9},{9,17},{17,25},{26,2},{2,... | collective-permute-start | bytes 1572872 | tf_op jit(solution)/shard_map/ppermute | solution.py:15
  3.6 36.5 %collective-permute-start.2 = (f32[256,512]{1,0:T(8,128)S(1)}, f32[256,512]{1,0:T(8,128)}, u32[]{:S(2)}, u32[]{:S(2)}) collective-permute-start(f32[256,512]{1,0:T(8,128)S(1)} %constant_dynamic-update-slice_fusion), channel_id=1, source_target_pairs={{16,0},{24,8},{0,16},{8,24},{17,1},{25,9},{1,17},{9,25},{18,2},{26... | collective-permute-start | bytes 1572872 | tf_op jit(solution)/shard_map/ppermute | solution.py:15
  6.2 45.7 %collective-permute-start.4 = (f32[256,512]{1,0:T(8,128)S(1)}, f32[256,512]{1,0:T(8,128)}, u32[]{:S(2)}, u32[]{:S(2)}) collective-permute-start(f32[256,512]{1,0:T(8,128)S(1)} %constant_dynamic-update-slice_fusion), channel_id=1, source_target_pairs={{0,1},{1,2},{2,3},{3,4},{4,5},{5,6},{6,7},{8,9},{9,10},{10,11},{11... | collective-permute-start | bytes 1572872 | tf_op jit(solution)/shard_map/ppermute | solution.py:21
  8.1 44.9 %collective-permute-start.5 = (f32[256,512]{1,0:T(8,128)S(1)}, f32[256,512]{1,0:T(8,128)S(1)}, u32[]{:S(2)}, u32[]{:S(2)}) collective-permute-start(f32[256,512]{1,0:T(8,128)S(1)} %constant_dynamic-update-slice_fusion), channel_id=1, source_target_pairs={{0,2},{1,3},{2,4},{3,5},{4,6},{5,7},{8,10},{9,11},{10,12},{11,13},... | collective-permute-start | bytes 1572872 | tf_op jit(solution)/shard_map/ppermute | solution.py:21
  11.5 41.5 %collective-permute-start.6 = (f32[256,512]{1,0:T(8,128)S(1)}, f32[256,512]{1,0:T(8,128)S(1)}, u32[]{:S(2)}, u32[]{:S(2)}) collective-permute-start(f32[256,512]{1,0:T(8,128)S(1)} %constant_dynamic-update-slice_fusion), channel_id=1, source_target_pairs={{0,4},{1,5},{2,6},{3,7},{8,12},{9,13},{10,14},{11,15},{16,20},{17,... | collective-permute-start | bytes 1572872 | tf_op jit(solution)/shard_map/ppermute | solution.py:21
  19.2 22.9 %collective-permute-start.1 = (f32[256,512]{1,0:T(8,128)}, f32[256,512]{1,0:T(8,128)}, u32[]{:S(2)}, u32[]{:S(2)}) collective-permute-start(f32[256,512]{1,0:T(8,128)} %collective-permute-done), channel_id=1, source_target_pairs={{0,1},{1,2},{2,3},{3,4},{4,5},{5,6},{6,7},{8,9},{9,10},{10,11},{11... | collective-permute-start | bytes 1572872 | tf_op jit(solution)/shard_map/ppermute | solution.py:21
  25.5 35.4 %copy-start.2 = (pred[128,1024]{0,1:T(8,128)(4,1)}, pred[128,1024]{0,1:T(8,128)(4,1)S(1)}, u32[]{:S(2)}) copy-start(pred[128,1024]{0,1:T(8,128)(4,1)S(1)} %get-tuple-element.25) | copy-start | bytes 393220
  40.1 11.6 %collective-permute-start.3 = (f32[256,512]{1,0:T(8,128)}, f32[256,512]{1,0:T(8,128)S(1)}, u32[]{:S(2)}, u32[]{:S(2)}) collective-permute-start(f32[256,512]{1,0:T(8,128)} %collective-permute-done.2), channel_id=1, source_target_pairs={{0,1},{1,2},{2,3},{3,4},{4,5},{5,6},{6,7},{8,9},{9,10},{10,11},{11... | collective-permute-start | bytes 1572872 | tf_op jit(solution)/shard_map/ppermute | solution.py:21
  53.0 4.4 %copy-start.4 = (f32[128,768]{0,1:T(8,128)S(1)}, f32[128,768]{0,1:T(8,128)}, u32[]{:S(2)}) copy-start(f32[128,768]{0,1:T(8,128)} %copy.75) | copy-start | bytes 1179652
  53.1 1.3 %copy-start.6 = (f32[1024,512]{1,0:T(8,128)}, f32[1024,512]{1,0:T(8,128)S(1)}, u32[]{:S(2)}) copy-start(f32[1024,512]{1,0:T(8,128)S(1)} %get-tuple-element.14) | copy-start | bytes 6291460
  53.1 7.8 %copy-start.5 = (f32[1024,512]{1,0:T(8,128)}, f32[1024,512]{1,0:T(8,128)S(1)}, u32[]{:S(2)}) copy-start(f32[1024,512]{1,0:T(8,128)S(1)} %get-tuple-element.13) | copy-start | bytes 6291460
  66.2 1.6 %copy-start.3 = (pred[128,1024]{0,1:T(8,128)(4,1)S(1)}, pred[128,1024]{0,1:T(8,128)(4,1)}, u32[]{:S(2)}) copy-start(pred[128,1024]{0,1:T(8,128)(4,1)} %copy-done.2) | copy-start | bytes 393220
  72.3 6.0 %copy-start.1 = (pred[128,1024]{0,1:T(8,128)(4,1)S(1)}, pred[128,1024]{0,1:T(8,128)(4,1)}, u32[]{:S(2)}) copy-start(pred[128,1024]{0,1:T(8,128)(4,1)} %get-tuple-element.26) | copy-start | bytes 393220
  89.8 5.5 %copy-start = (f32[128,768]{1,0:T(8,128)S(1)}, f32[128,768]{1,0:T(8,128)}, u32[]{:S(2)}) copy-start(f32[128,768]{1,0:T(8,128)} %copy.46) | copy-start | bytes 1179652
where the time goes:
time: 98.6 us; the launch traced here: 97.8 us
  matrix products  31.6 us (32%)
  waiting for transfers between devices  23.1 us (23%)
  local copies, waits for them, and re-layouts  18.5 us (19%)
  starting transfers between devices  14.8 us (15%)
  other arithmetic  9.55 us (10%)
    dot_general x4, matrix products, body(): jnp.einsum('grk,kd->rgd', weights, value_portion, precision=lax.Precision...  16.5 us
    dot_general x4, matrix products, body(): jnp.einsum('rgd,kd->grk', query_portion, key_portion, precision=lax.Preci...  15.1 us
    ppermute x2, waiting for transfers between devices, shifted(): return lax.ppermute(block, axis, route)  14.6 us
    ppermute x5, starting transfers between devices, shifted_2(): return lax.ppermute(block, axis, route)  10.5 us
    ppermute x5, waiting for transfers between devices, shifted_2(): return lax.ppermute(block, axis, route)  8.46 us
    reshape x4, local copies, waits for them, and re-layouts, body(): (weighted / jnp.transpose(denominator)[:, :, None]).reshape(BLOCK_TOKENS,...  6.94 us
    unnamed x28, local copies, waits for them, and re-layouts  5.77 us
    ppermute x2, starting transfers between devices, shifted(): return lax.ppermute(block, axis, route)  4.22 us
  transfers between devices with their start and end apart: 7, of which 2 were waited for; matrix products, arithmetic and copies ran while one was open for 13% of the time, Pallas kernels for 0%

commit v1 on v0

v1 whole, which is shorter than its diff:
```python
import functools
import math

import jax
import jax.numpy as jnp
from jax import lax
from jax.experimental import pallas as pl
from jax.experimental.pallas import tpu as pltpu
from jax.sharding import PartitionSpec as P

QUERY_HEADS = 12
KEY_VALUE_HEADS = 2
HEAD_FEATURES = 128
BLOCK_TOKENS = 128
STEP_HEADS = 3
SCALE = HEAD_FEATURES ** (-0.5) * math.log2(math.e)
F32, BF16 = jnp.float32, jnp.bfloat16


def split(x):
    high = x.astype(BF16)
    return high, (x - high.astype(F32)).astype(BF16)


def attend_kernel(near, far, first, last, *refs):
    refs = list(refs)
    lists_ref, q_ref = refs.pop(0), refs.pop(0)
    near_refs = [(refs.pop(0), refs.pop(0)) for _ in near]
    far_refs = [(refs.pop(0), refs.pop(0)) for _ in far]
    if not first:
        acc_in, stat_in = refs.pop(0), refs.pop(0)
    out_ref = refs.pop(0)
    if not last:
        stat_out = refs.pop(0)

    local_block = pl.program_id(0)
    blocks = pl.num_programs(0)
    device = lax.axis_index("ctxhi") * lax.axis_size("ctxlo") + lax.axis_index("ctxlo")
    slots = lists_ref.shape[1]

    def bias(key_block):
        hit = lists_ref[local_block, 0] == key_block
        for slot in range(1, slots):
            hit = hit | (lists_ref[local_block, slot] == key_block)
        return jnp.where(hit & (key_block >= 0), 0.0, -jnp.inf).astype(F32)

    rows = STEP_HEADS * BLOCK_TOKENS
    queries = jnp.concatenate(
        [q_ref[:, h * HEAD_FEATURES : (h + 1) * HEAD_FEATURES] for h in range(STEP_HEADS)], axis=0
    )
    q_high, q_low = split(queries * SCALE)
    q_terms = jnp.concatenate([q_high, q_low, q_high], axis=1)

    def scores_of(keys):
        k_high, k_low = split(keys)
        k_terms = jnp.concatenate([k_high, k_high, k_low], axis=1)
        return lax.dot_general(q_terms, k_terms, (((1,), (1,)), ((), ())), preferred_element_type=F32)

    scores, values = [], []
    for offset, (k_ref, v_ref) in zip(near, near_refs):
        keys = k_ref.shape[0]
        part = scores_of(k_ref[...])
        col = lax.broadcasted_iota(jnp.int32, (1, keys), 1)
        base = (device - offset) * blocks
        shift = jnp.full((1, keys), bias(base), F32)
        for b in range(1, keys // BLOCK_TOKENS):
            shift = jnp.where(col >= b * BLOCK_TOKENS, bias(base + b), shift)
        part = part + shift
        if offset == 0:
            row = lax.broadcasted_iota(jnp.int32, (rows, keys), 0) % BLOCK_TOKENS
            col = lax.broadcasted_iota(jnp.int32, (rows, keys), 1)
            part = jnp.where(col - row <= local_block * BLOCK_TOKENS, part, -jnp.inf)
        scores.append(part)
        values.append(v_ref[...])
    if far:
        keys = jnp.concatenate([k_ref[...] for k_ref, _ in far_refs], axis=0)
        part = scores_of(keys)
        shift = jnp.concatenate(
            [
                jnp.full((1, BLOCK_TOKENS), bias((device - offset) * blocks + local_block), F32)
                for offset in far
            ],
            axis=1,
        )
        scores.append(part + shift)
        values.append(jnp.concatenate([v_ref[...] for _, v_ref in far_refs], axis=0))
    scores = jnp.concatenate(scores, axis=1)
    values = jnp.concatenate(values, axis=0)

    peak = jnp.max(scores, axis=1, keepdims=True)
    if not first:
        old_peak = jnp.concatenate([stat_in[0, :, h : h + 1] for h in range(STEP_HEADS)], axis=0)
        old_total = jnp.concatenate(
            [stat_in[0, :, STEP_HEADS + h : STEP_HEADS + h + 1] for h in range(STEP_HEADS)], axis=0
        )
        peak = jnp.maximum(peak, old_peak)
        fade = jnp.exp2(old_peak - peak)
    weights = jnp.exp2(scores - peak)
    total = jnp.sum(weights, axis=1, keepdims=True)
    w_high, w_low = split(weights)
    v_high, v_low = split(values)
    v_terms = jnp.concatenate([v_high, v_low], axis=1)
    both = jnp.dot(
        jnp.concatenate([w_high, w_low], axis=1),
        jnp.concatenate([v_terms, v_terms], axis=0),
        preferred_element_type=F32,
    )
    acc = both[:, :HEAD_FEATURES] + both[:, HEAD_FEATURES:]
    if not first:
        total = total + old_total * fade
        old = jnp.concatenate(
            [acc_in[:, h * HEAD_FEATURES : (h + 1) * HEAD_FEATURES] for h in range(STEP_HEADS)], axis=0
        )
        acc = acc + old * fade
    if last:
        acc = acc / total
    for h in range(STEP_HEADS):
        out_ref[:, h * HEAD_FEATURES : (h + 1) * HEAD_FEATURES] = acc[
            h * BLOCK_TOKENS : (h + 1) * BLOCK_TOKENS
        ]
    if not last:
        lane = lax.broadcasted_iota(jnp.int32, (BLOCK_TOKENS, HEAD_FEATURES), 1)
        stat = jnp.zeros((BLOCK_TOKENS, HEAD_FEATURES), F32)
        for h in range(STEP_HEADS):
            cut = slice(h * BLOCK_TOKENS, (h + 1) * BLOCK_TOKENS)
            stat = jnp.where(lane == h, peak[cut], stat)
            stat = jnp.where(lane == STEP_HEADS + h, total[cut], stat)
        stat_out[0] = stat


def attend(lists, query, near, far, carry, last, name):
    tokens, width = query.shape
    blocks = tokens // BLOCK_TOKENS
    steps = QUERY_HEADS // STEP_HEADS
    per_group = QUERY_HEADS // KEY_VALUE_HEADS // STEP_HEADS
    cols = STEP_HEADS * HEAD_FEATURES
    first = carry is None
    part = pl.BlockSpec((BLOCK_TOKENS, cols), lambda b, s: (b, s))
    stat = pl.BlockSpec((1, BLOCK_TOKENS, HEAD_FEATURES), lambda b, s: (b * steps + s, 0, 0))
    specs = [pl.BlockSpec(memory_space=pltpu.SMEM), part]
    operands = [lists, query]
    for shard in near.values():
        specs.append(pl.BlockSpec((tokens, HEAD_FEATURES), lambda b, s: (0, s // per_group)))
        specs.append(
            pl.BlockSpec((tokens, HEAD_FEATURES), lambda b, s: (0, KEY_VALUE_HEADS + s // per_group))
        )
        operands += [shard, shard]
    for shard in far.values():
        specs.append(pl.BlockSpec((BLOCK_TOKENS, HEAD_FEATURES), lambda b, s: (b, s // per_group)))
        specs.append(
            pl.BlockSpec(
                (BLOCK_TOKENS, HEAD_FEATURES), lambda b, s: (b, KEY_VALUE_HEADS + s // per_group)
            )
        )
        operands += [shard, shard]
    if not first:
        specs += [part, stat]
        operands += list(carry)
    out_shape = [jax.ShapeDtypeStruct((tokens, width), F32)]
    out_specs = [part]
    if not last:
        out_shape.append(jax.ShapeDtypeStruct((blocks * steps, BLOCK_TOKENS, HEAD_FEATURES), F32))
        out_specs.append(stat)
    keys = len(near) * tokens + len(far) * BLOCK_TOKENS
    pairs = tokens * QUERY_HEADS * keys
    return pl.pallas_call(
        functools.partial(attend_kernel, tuple(near), tuple(far), first, last),
        grid=(blocks, steps),
        in_specs=specs,
        out_specs=out_specs,
        out_shape=out_shape,
        compiler_params=pltpu.CompilerParams(
            dimension_semantics=("arbitrary", "arbitrary"), vmem_limit_bytes=32 * 2**20
        ),
        cost_estimate=pl.CostEstimate(
            flops=pairs * HEAD_FEATURES * 16, bytes_accessed=4 * tokens * width * 4, transcendentals=pairs
        ),
        name=name,
    )(*operands)


def body(query_matrix, key_matrix, value_matrix, block_lists):
    blocks = query_matrix.shape[0] // BLOCK_TOKENS
    inner = lax.axis_size("ctxlo")
    outer = lax.axis_size("ctxhi")
    devices = inner * outer
    device = lax.axis_index("ctxhi") * inner + lax.axis_index("ctxlo")

    def place(shard):
        return shard % inner * outer + shard // inner

    def move(block, pairs):
        return lax.ppermute(block, ("ctxlo", "ctxhi"), [(place(a), place(b)) for a, b in pairs])

    def shifted(block, offset):
        return move(block, [(i, i + offset) for i in range(devices - offset)])

    own = jnp.concatenate([key_matrix, value_matrix], axis=1)
    far_offsets = sorted(
        {2**j // blocks for j in range(2, 40) if 2**j < devices * blocks and 2**j // blocks > 2}
    )
    shards = {1: shifted(own, 1)}
    for offset in reversed(far_offsets):
        if offset == inner and 2 * offset in shards:
            odd = device // inner % 2 == 1
            give = jnp.where(odd, shards[2 * offset], own)
            shards[offset] = move(give, [(i, i ^ inner) for i in range(devices)])
        else:
            shards[offset] = shifted(own, offset)
    shards[2] = shifted(shards[1], 1)

    early = far_offsets[-1:]
    late = far_offsets[:-1]
    carry = attend(block_lists, query_matrix, {0: own}, {}, None, False, "own")
    carry = attend(
        block_lists, query_matrix, {1: shards[1]}, {o: shards[o] for o in early}, carry, False, "early"
    )
    return attend(
        block_lists, query_matrix, {2: shards[2]}, {o: shards[o] for o in late}, carry, True, "late"
    )[0]


def solution(mesh):
    spec = P(("ctxhi", "ctxlo"), None)
    return jax.shard_map(
        body, mesh=mesh, in_specs=(spec,) * 4, out_specs=spec, check_vma=False
    )
```

time: 98.6 us -> 63.4 us (0.64)
  Pallas kernels: 0 us -> 31.9 us
  matrix products: 31.6 us -> 0 us
  local copies, waits for them, and re-layouts: 18.5 us -> 2.07 us
  other arithmetic: 9.55 us -> 0.08 us
  starting transfers between devices: 14.8 us -> 10.2 us
  waiting for transfers between devices: 23.1 us -> 18.5 us
    pallas_call x0 -> x3, Pallas kernels: none -> 31.9 us  [attend(): pl.pallas_call(functools.partial(attend_kernel, tuple(near), tuple(far),...]
    dot_general x8 -> x0, matrix products: 31.6 us -> none  [the longest x4 16.5 us: body(): jnp.einsum('grk,kd->rgd', weights, value_portion, precision=lax.Precision...]
    reshape x4 -> x0, local copies, waits for them, and re-layouts: 6.94 us -> none  [body(): (weighted / jnp.transpose(denominator)[:, :, None]).reshape(BLOCK_TOKENS,...]
    unnamed x28 -> x5, local copies, waits for them, and re-layouts: 5.77 us -> 1.1 us
    ppermute x7 -> x5, starting transfers between devices: 14.8 us -> 10.2 us  [move(): lax.ppermute(block, ('ctxlo', 'ctxhi'), [(place(a), place(b)) for a, b in...]
    ppermute x7 -> x5, waiting for transfers between devices: 23.1 us -> 18.5 us  [move(): lax.ppermute(block, ('ctxlo', 'ctxhi'), [(place(a), place(b)) for a, b in...]
    and x2 -> x0, other arithmetic: 2.71 us -> none  [the longest x1 2.04 us: body(): listed[None, :, None] & ((distance_array[None, :, None] > 0) | causal)]
    concatenate x1 -> x0, other arithmetic: 2.45 us -> none  [body(): return jnp.concatenate(outputs, axis=0)]
  transfers between devices with their start and end apart: 7 -> 5, of which waited for: 2 -> 3; matrix products, arithmetic and copies ran while one was open for 13% -> 0% of each run, Pallas kernels for 0% -> 29%
where the time goes in v1:
time: 63.4 us; the launch traced here: 62.9 us
  Pallas kernels  31.9 us (50%)
  waiting for transfers between devices  18.5 us (29%)
  starting transfers between devices  10.2 us (16%)
  local copies, waits for them, and re-layouts  2.07 us (3%)
    pallas_call x3, Pallas kernels, attend(): pl.pallas_call(functools.partial(attend_kernel, tuple(near), tuple(far),...  31.9 us
    ppermute x5, waiting for transfers between devices, move(): lax.ppermute(block, ('ctxlo', 'ctxhi'), [(place(a), place(b)) for a, b in...  18.5 us
    ppermute x5, starting transfers between devices, move(): lax.ppermute(block, ('ctxlo', 'ctxhi'), [(place(a), place(b)) for a, b in...  10.2 us
  transfers between devices with their start and end apart: 5, of which 3 were waited for; matrix products, arithmetic and copies ran while one was open for 0% of the time, Pallas kernels for 29%

profile of v1, /device:TPU:4, one launch (start us, length us, event | category | flops | bytes accessed | tf_op | source)
XLA Modules:
  0.0 62.9 jit_solution(17066277409800871367)
XLA Ops:
  0.0 0.0 copy-start
  0.0 0.0 copy-start.1
  0.0 1.1 %constant_dynamic-update-slice_fusion.1 = f32[256,512]{1,0:T(8,128)S(1)} fusion(f32[256,256]{1,0:T(8,128)} %param.5), kind=kLoop, calls=%fused_computation.2 | loop fusion | bytes 524288
  1.1 1.0 %constant_dynamic-update-slice_fusion.refs_2_.refs_3_ = f32[256,512]{1,0:T(8,128)S(1)} fusion(f32[256,512]{1,0:T(8,128)S(1)} %constant_dynamic-update-slice_fusion.1, f32[256,256]{1,0:T(8,128)} %param.6), kind=kLoop, calls=%fused_computation.1 | loop fusion | bytes 524288 | tf_op jit(solution)/shard_map/concatenate | solution.py:198
  2.1 3.4 %collective-permute-start.2 = (f32[256,512]{1,0:T(8,128)S(1)}, f32[256,512]{1,0:T(8,128)S(1)}, u32[]{:S(2)}, u32[]{:S(2)}) collective-permute-start(f32[256,512]{1,0:T(8,128)S(1)} %constant_dynamic-update-slice_fusion.refs_2_.refs_3_), channel_id=1, source_target_pairs={{0,2},{8,10},{16,18},{24,26},{1,3},{9,11},{17,19},{25,27},{2,4},{1... | collective-permute-start | bytes 1572872 | tf_op jit(solution)/shard_map/ppermute | solution.py:193
  5.5 3.5 %collective-permute-start = (f32[256,512]{1,0:T(8,128)S(1)}, f32[256,512]{1,0:T(8,128)S(1)}, u32[]{:S(2)}, u32[]{:S(2)}) collective-permute-start(f32[256,512]{1,0:T(8,128)S(1)} %constant_dynamic-update-slice_fusion.refs_2_.refs_3_), channel_id=1, source_target_pairs={{0,8},{8,16},{16,24},{24,1},{1,9},{9,17},{17,25},{25,2},{2,10},{10... | collective-permute-start | bytes 1572872 | tf_op jit(solution)/shard_map/ppermute | solution.py:193
  9.0 1.3 %collective-permute-start.4 = (f32[256,512]{1,0:T(8,128)S(1)}, f32[256,512]{1,0:T(8,128)}, u32[]{:S(2)}, u32[]{:S(2)}) collective-permute-start(f32[256,512]{1,0:T(8,128)S(1)} %constant_dynamic-update-slice_fusion.refs_2_.refs_3_), channel_id=1, source_target_pairs={{0,4},{8,12},{16,20},{24,28},{1,5},{9,13},{17,21},{25,29},{2,6},{1... | collective-permute-start | bytes 1572872 | tf_op jit(solution)/shard_map/ppermute | solution.py:193
  10.3 12.9 %collective-permute-done.2.refs_6_.refs_7_ = f32[256,512]{1,0:T(8,128)S(1)} collective-permute-done((f32[256,512]{1,0:T(8,128)S(1)}, f32[256,512]{1,0:T(8,128)S(1)}, u32[]{:S(2)}, u32[]{:S(2)}) %collective-permute-start.2) | collective-permute-done | bytes 524320 | tf_op jit(solution)/shard_map/ppermute | solution.py:193
  23.3 0.1 broadcast_select_fusion
  23.3 0.1 collective-permute-start.3
  23.4 1.2 %collective-permute-done.refs_2_.refs_3_ = f32[256,512]{1,0:T(8,128)S(1)} collective-permute-done((f32[256,512]{1,0:T(8,128)S(1)}, f32[256,512]{1,0:T(8,128)S(1)}, u32[]{:S(2)}, u32[]{:S(2)}) %collective-permute-start) | collective-permute-done | bytes 524320 | tf_op jit(solution)/shard_map/ppermute | solution.py:193
  24.7 1.9 %collective-permute-start.1 = (f32[256,512]{1,0:T(8,128)S(1)}, f32[256,512]{1,0:T(8,128)S(1)}, u32[]{:S(2)}, u32[]{:S(2)}) collective-permute-start(f32[256,512]{1,0:T(8,128)S(1)} %collective-permute-done.refs_2_.refs_3_), channel_id=1, source_target_pairs={{0,8},{8,16},{16,24},{24,1},{1,9},{9,17},{17,25},{25,2},{2,10},{10... | collective-permute-start | bytes 1572872 | tf_op jit(solution)/shard_map/ppermute | solution.py:193
  26.6 0.0 copy-done
  26.6 0.0 copy-done.1
  26.6 6.9 %own.1 = (f32[256,1536]{1,0:T(8,128)S(1)}, f32[8,128,128]{2,1,0:T(8,128)S(1)}) custom-call(s32[2,15]{1,0:T(2,128)S(1)} %copy-done.1, f32[256,1536]{1,0:T(8,128)S(1)} %copy-done, f32[256,512]{1,0:T(8,128)S(1)} %constant_dynamic-update-slice_fusion.refs_2_.refs_3_, f32[256,512]{1,0:T(8,128)S(1)} %constant_dynamic-update-slice_fusion.refs_2_.refs_3_), custom_call_target="tpu_custom_call" | custom-call | flops 1610612736 | bytes 6291456 | tf_op jit(solution)/shard_map/own/pallas_call | solution.py:166
  33.5 4.3 %collective-permute-done.4.refs_4_.refs_5_ = f32[256,512]{1,0:T(8,128)} collective-permute-done((f32[256,512]{1,0:T(8,128)S(1)}, f32[256,512]{1,0:T(8,128)}, u32[]{:S(2)}, u32[]{:S(2)}) %collective-permute-start.4) | collective-permute-done | bytes 524320 | tf_op jit(solution)/shard_map/ppermute | solution.py:193
  37.8 11.7 %early.1 = (f32[256,1536]{1,0:T(8,128)S(1)}, f32[8,128,128]{2,1,0:T(8,128)S(1)}) custom-call(s32[2,15]{1,0:T(2,128)S(1)} %copy-done.1, f32[256,1536]{1,0:T(8,128)S(1)} %copy-done, f32[256,512]{1,0:T(8,128)S(1)} %collective-permute-done.refs_2_.refs_3_, f32[256,512]{1,0:T(8,128)S(1)} %collective-permute-done.refs_2_.refs_3_, ...), custom_call_target="tpu_custom_call" | custom-call | flops 2415919104 | bytes 6291456 | tf_op jit(solution)/shard_map/early/pallas_call | solution.py:166
  49.5 0.0 collective-permute-done.3.refs_4_.refs_5_
  49.5 0.0 collective-permute-done.1.refs_2_.refs_3_
  49.5 13.4 %late.1 = f32[256,1536]{1,0:T(8,128)} custom-call(s32[2,15]{1,0:T(2,128)S(1)} %copy-done.1, f32[256,1536]{1,0:T(8,128)S(1)} %copy-done, f32[256,512]{1,0:T(8,128)S(1)} %collective-permute-done.1.refs_2_.refs_3_, f32[256,512]{1,0:T(8,128)S(1)} %collective-permute-done.1.refs_2_.refs_3_, f32[256,512]{1,0:T(8,128)S(1)} %collective-permute-done.3.refs_4_.refs_5_, ...), custom_call_target="tpu_custom_call" | custom-call | flops 3221225472 | bytes 6291456 | tf_op jit(solution)/shard_map/late/pallas_call | solution.py:166
Async XLA Ops:
  0.0 26.6 %copy-start = (f32[256,1536]{1,0:T(8,128)S(1)}, f32[256,1536]{1,0:T(8,128)}, u32[]{:S(2)}) copy-start(f32[256,1536]{1,0:T(8,128)} %refs_1_.5) | copy-start | bytes 4718596
  0.0 26.6 %copy-start.1 = (s32[2,15]{1,0:T(2,128)S(1)}, s32[2,15]{1,0:T(2,128)}, u32[]{:S(2)}) copy-start(s32[2,15]{1,0:T(2,128)} %refs_0_.5) | copy-start | bytes 364
  2.1 21.2 %collective-permute-start.2 = (f32[256,512]{1,0:T(8,128)S(1)}, f32[256,512]{1,0:T(8,128)S(1)}, u32[]{:S(2)}, u32[]{:S(2)}) collective-permute-start(f32[256,512]{1,0:T(8,128)S(1)} %constant_dynamic-update-slice_fusion.refs_2_.refs_3_), channel_id=1, source_target_pairs={{0,2},{8,10},{16,18},{24,26},{1,3},{9,11},{17,19},{25,27},{2,4},{1... | collective-permute-start | bytes 1572872 | tf_op jit(solution)/shard_map/ppermute | solution.py:193
  5.5 19.2 %collective-permute-start = (f32[256,512]{1,0:T(8,128)S(1)}, f32[256,512]{1,0:T(8,128)S(1)}, u32[]{:S(2)}, u32[]{:S(2)}) collective-permute-start(f32[256,512]{1,0:T(8,128)S(1)} %constant_dynamic-update-slice_fusion.refs_2_.refs_3_), channel_id=1, source_target_pairs={{0,8},{8,16},{16,24},{24,1},{1,9},{9,17},{17,25},{25,2},{2,10},{10... | collective-permute-start | bytes 1572872 | tf_op jit(solution)/shard_map/ppermute | solution.py:193
  9.0 28.8 %collective-permute-start.4 = (f32[256,512]{1,0:T(8,128)S(1)}, f32[256,512]{1,0:T(8,128)}, u32[]{:S(2)}, u32[]{:S(2)}) collective-permute-start(f32[256,512]{1,0:T(8,128)S(1)} %constant_dynamic-update-slice_fusion.refs_2_.refs_3_), channel_id=1, source_target_pairs={{0,4},{8,12},{16,20},{24,28},{1,5},{9,13},{17,21},{25,29},{2,6},{1... | collective-permute-start | bytes 1572872 | tf_op jit(solution)/shard_map/ppermute | solution.py:193
  23.3 26.1 %collective-permute-start.3 = (f32[256,512]{1,0:T(8,128)S(1)}, f32[256,512]{1,0:T(8,128)S(1)}, u32[]{:S(2)}, u32[]{:S(2)}) collective-permute-start(f32[256,512]{1,0:T(8,128)S(1)} %broadcast_select_fusion), channel_id=1, source_target_pairs={{0,1},{8,9},{16,17},{24,25},{1,0},{9,8},{17,16},{25,24},{2,3},{10,... | collective-permute-start | bytes 1572872 | tf_op jit(solution)/shard_map/ppermute | solution.py:193
  24.7 24.8 %collective-permute-start.1 = (f32[256,512]{1,0:T(8,128)S(1)}, f32[256,512]{1,0:T(8,128)S(1)}, u32[]{:S(2)}, u32[]{:S(2)}) collective-permute-start(f32[256,512]{1,0:T(8,128)S(1)} %collective-permute-done.refs_2_.refs_3_), channel_id=1, source_target_pairs={{0,8},{8,16},{16,24},{24,1},{1,9},{9,17},{17,25},{25,2},{2,10},{10... | collective-permute-start | bytes 1572872 | tf_op jit(solution)/shard_map/ppermute | solution.py:193

commit v2 on v1

v2 whole, which is shorter than its diff:
```python
import functools
import math

import jax
import jax.numpy as jnp
from jax import lax
from jax.experimental import pallas as pl
from jax.experimental.pallas import tpu as pltpu
from jax.sharding import PartitionSpec as P

QUERY_HEADS = 12
KEY_VALUE_HEADS = 2
HEAD_FEATURES = 128
BLOCK_TOKENS = 128
CHAIN_HEADS = 3
CHAIN_ROWS = CHAIN_HEADS * BLOCK_TOKENS
CHAIN_COLS = CHAIN_HEADS * HEAD_FEATURES
SCALE = HEAD_FEATURES ** (-0.5) * math.log2(math.e)
F32, BF16 = jnp.float32, jnp.bfloat16


def split(x):
    high = x.astype(BF16)
    return high, (x - high.astype(F32)).astype(BF16)


def attend_kernel(near, far, first, last, *refs):
    refs = list(refs)
    lists_ref, q_ref = refs.pop(0), refs.pop(0)
    near_refs = [refs.pop(0) for _ in near]
    far_refs = [refs.pop(0) for _ in far]
    if not first:
        acc_in, peak_in, total_in = refs.pop(0), refs.pop(0), refs.pop(0)
    if last:
        out_hbm = refs.pop(0)
    else:
        acc_out, peak_out, total_out = refs.pop(0), refs.pop(0), refs.pop(0)
    scores = (refs.pop(0), refs.pop(0))
    weights = (refs.pop(0), refs.pop(0))
    fades = (refs.pop(0), refs.pop(0))
    k_near = v_near = k_far = v_far = None
    if near:
        k_near, v_near = refs.pop(0), refs.pop(0)
    if far:
        k_far, v_far = refs.pop(0), refs.pop(0)
    if last:
        acc_out, out_sem = refs.pop(0), refs.pop(0)

    tokens = q_ref.shape[0]
    blocks = tokens // BLOCK_TOKENS
    groups = KEY_VALUE_HEADS
    steps = blocks * groups
    slots = lists_ref.shape[1]
    device = lax.axis_index("ctxhi") * lax.axis_size("ctxlo") + lax.axis_index("ctxlo")
    near_keys = len(near) * tokens
    keys = near_keys + len(far) * BLOCK_TOKENS

    def prepare(kv, g, k_terms, v_terms, index, at):
        rows = kv.shape[0]
        high, low = split(kv[:, g * HEAD_FEATURES : (g + 1) * HEAD_FEATURES])
        k_terms[index, at : at + rows, :] = jnp.concatenate([high, high, low], axis=1)
        v = groups + g
        terms = jnp.concatenate(split(kv[:, v * HEAD_FEATURES : (v + 1) * HEAD_FEATURES]), axis=1)
        v_terms[index, 2 * at : 2 * at + rows, :] = terms
        v_terms[index, 2 * at + rows : 2 * (at + rows), :] = terms

    for g in range(groups):
        for n, ref in enumerate(near_refs):
            prepare(ref, g, k_near, v_near, g, n * tokens)
        for b in range(blocks):
            for n, ref in enumerate(far_refs):
                block = ref.at[b * BLOCK_TOKENS : (b + 1) * BLOCK_TOKENS]
                prepare(block, g, k_far, v_far, b * groups + g, n * BLOCK_TOKENS)

    def place(step, half):
        block, group = step // groups, step % groups
        row = pl.multiple_of(block * BLOCK_TOKENS, BLOCK_TOKENS)
        chain = group * 2 + half
        col = pl.multiple_of(chain * CHAIN_COLS, HEAD_FEATURES)
        stat = pl.multiple_of((block * QUERY_HEADS + chain * CHAIN_HEADS) * BLOCK_TOKENS, BLOCK_TOKENS)
        return block, group, row, col, stat

    def score(step, half):
        block, group, row, col, _ = place(step, half)
        q = jnp.concatenate(
            [
                q_ref[pl.ds(row, BLOCK_TOKENS), pl.ds(col + h * HEAD_FEATURES, HEAD_FEATURES)]
                for h in range(CHAIN_HEADS)
            ],
            axis=0,
        )
        high, low = split(q * SCALE)
        terms = jnp.concatenate([high, low, high], axis=1)
        dims = (((1,), (1,)), ((), ()))
        if near:
            scores[half][:, :near_keys] = lax.dot_general(
                terms, k_near[group], dims, preferred_element_type=F32
            )
        if far:
            scores[half][:, near_keys:] = lax.dot_general(
                terms, k_far[step], dims, preferred_element_type=F32
            )

    def soften(step, half):
        block, group, _, _, stat = place(step, half)

        def bias(key_block):
            hit = lists_ref[block, 0] == key_block
            for slot in range(1, slots):
                hit = hit | (lists_ref[block, slot] == key_block)
            return jnp.where(hit & (key_block >= 0), 0.0, -jnp.inf).astype(F32)

        ids = []
        for offset in near:
            ids += [(device - offset) * blocks + b for b in range(blocks)]
        ids += [(device - offset) * blocks + block for offset in far]
        biases = [bias(i) for i in ids]
        square = (BLOCK_TOKENS, BLOCK_TOKENS)
        for h in range(CHAIN_HEADS):
            rows = slice(h * BLOCK_TOKENS, (h + 1) * BLOCK_TOKENS)
            tiles = []
            for n, shift in enumerate(biases):
                tile = scores[half][rows, n * BLOCK_TOKENS : (n + 1) * BLOCK_TOKENS] + shift
                if near and near[n // blocks] == 0 if n * BLOCK_TOKENS < near_keys else False:
                    ahead = lax.broadcasted_iota(jnp.int32, square, 1) - lax.broadcasted_iota(
                        jnp.int32, square, 0
                    )
                    tile = jnp.where(ahead <= (block - n % blocks) * BLOCK_TOKENS, tile, -jnp.inf)
                tiles.append(tile)
            peak = jnp.max(functools.reduce(jnp.maximum, tiles), axis=1, keepdims=True)
            peak = jnp.broadcast_to(peak, square)
            at = pl.ds(stat + h * BLOCK_TOKENS, BLOCK_TOKENS)
            if not first:
                old = peak_in[at, :]
                peak = jnp.maximum(peak, old)
                fade = jnp.exp2(old - peak)
            parts = [jnp.exp2(tile - peak) for tile in tiles]
            total = functools.reduce(jnp.add, parts)
            if not first:
                total = total + total_in[at, :] * fade
            if last:
                inverse = jnp.broadcast_to(1.0 / jnp.sum(total, axis=1, keepdims=True), square)
                fades[half][rows, :BLOCK_TOKENS] = fade
                fades[half][rows, BLOCK_TOKENS:] = inverse
            else:
                if not first:
                    fades[half][rows, :BLOCK_TOKENS] = fade
                peak_out[at, :] = peak
                total_out[at, :] = total
            for n, part in enumerate(parts):
                start = n * BLOCK_TOKENS
                if start < near_keys:
                    base, size = start // tokens * tokens, tokens
                else:
                    base, size = start, BLOCK_TOKENS
                high, low = split(part)
                here = start + base
                weights[half][rows, here : here + BLOCK_TOKENS] = high
                weights[half][rows, here + size : here + size + BLOCK_TOKENS] = low

    def gather(step, half):
        block, group, row, col, _ = place(step, half)
        both = None
        if near:
            both = jnp.dot(
                weights[half][:, : 2 * near_keys], v_near[group], preferred_element_type=F32
            )
        if far:
            more = jnp.dot(weights[half][:, 2 * near_keys :], v_far[step], preferred_element_type=F32)
            both = more if both is None else both + more
        acc = both[:, :HEAD_FEATURES] + both[:, HEAD_FEATURES:]
        for h in range(CHAIN_HEADS):
            rows = slice(h * BLOCK_TOKENS, (h + 1) * BLOCK_TOKENS)
            at = (pl.ds(row, BLOCK_TOKENS), pl.ds(col + h * HEAD_FEATURES, HEAD_FEATURES))
            part = acc[rows]
            if not first:
                part = part + acc_in[at] * fades[half][rows, :BLOCK_TOKENS]
            if last:
                part = part * fades[half][rows, BLOCK_TOKENS:]
            acc_out[at] = part

    def send(step):
        _, group, row, _, _ = place(step, 0)
        col = pl.multiple_of(group * 2 * CHAIN_COLS, HEAD_FEATURES)
        at = (pl.ds(row, BLOCK_TOKENS), pl.ds(col, 2 * CHAIN_COLS))
        return pltpu.make_async_copy(acc_out.at[at], out_hbm.at[at], out_sem.at[step])

    score(0, 0)

    @pl.loop(0, steps)
    def _(step):
        score(step, 1)
        soften(step, 0)
        gather(jnp.maximum(step - 1, 0), 1)
        score(jnp.minimum(step + 1, steps - 1), 0)
        soften(step, 1)
        gather(step, 0)
        if last:

            @pl.when(step > 0)
            def _():
                send(step - 1).start()

    gather(steps - 1, 1)
    if last:
        send(steps - 1).start()
        for step in range(steps):
            send(step).wait()


def attend(lists, query, near, far, carry, last, name):
    tokens, width = query.shape
    blocks = tokens // BLOCK_TOKENS
    steps = blocks * KEY_VALUE_HEADS
    first = carry is None
    vmem = pl.BlockSpec(memory_space=pltpu.VMEM)
    operands = [lists, query, *near.values(), *far.values()] + ([] if first else list(carry))
    specs = [pl.BlockSpec(memory_space=pltpu.SMEM)] + [vmem] * (len(operands) - 1)
    wide = jax.ShapeDtypeStruct((tokens, width), F32)
    stat = jax.ShapeDtypeStruct((tokens * QUERY_HEADS, BLOCK_TOKENS), F32)
    near_keys, far_keys = len(near) * tokens, len(far) * BLOCK_TOKENS
    keys = near_keys + far_keys
    scratch = [pltpu.VMEM((CHAIN_ROWS, keys), F32)] * 2
    scratch += [pltpu.VMEM((CHAIN_ROWS, 2 * keys), BF16)] * 2
    scratch += [pltpu.VMEM((CHAIN_ROWS, 2 * BLOCK_TOKENS), F32)] * 2
    for number, size in ((KEY_VALUE_HEADS, near_keys), (steps, far_keys)):
        if size:
            scratch.append(pltpu.VMEM((number, size, 3 * HEAD_FEATURES), BF16))
            scratch.append(pltpu.VMEM((number, 2 * size, 2 * HEAD_FEATURES), BF16))
    if last:
        scratch += [pltpu.VMEM((tokens, width), F32), pltpu.SemaphoreType.DMA((steps,))]
        out_shape, out_specs = wide, pl.BlockSpec(memory_space=pl.ANY)
    else:
        out_shape, out_specs = (wide, stat, stat), (vmem,) * 3
    pairs = tokens * QUERY_HEADS * keys
    return pl.pallas_call(
        functools.partial(attend_kernel, tuple(near), tuple(far), first, last),
        in_specs=specs,
        out_specs=out_specs,
        out_shape=out_shape,
        scratch_shapes=scratch,
        compiler_params=pltpu.CompilerParams(vmem_limit_bytes=VMEM_LIMIT),
        cost_estimate=pl.CostEstimate(
            flops=pairs * HEAD_FEATURES * 16, bytes_accessed=4 * tokens * width * 4, transcendentals=pairs
        ),
        name=name,
    )(*operands)


VMEM_LIMIT = 40 * 2**20

def body(query_matrix, key_matrix, value_matrix, block_lists):
    blocks = query_matrix.shape[0] // BLOCK_TOKENS
    inner = lax.axis_size("ctxlo")
    outer = lax.axis_size("ctxhi")
    devices = inner * outer
    device = lax.axis_index("ctxhi") * inner + lax.axis_index("ctxlo")

    def place(shard):
        return shard % inner * outer + shard // inner

    def move(block, pairs):
        return lax.ppermute(block, ("ctxlo", "ctxhi"), [(place(a), place(b)) for a, b in pairs])

    def shifted(block, offset):
        return move(block, [(i, i + offset) for i in range(devices - offset)])

    own = jnp.concatenate([key_matrix, value_matrix], axis=1)
    far_offsets = sorted(
        {2**j // blocks for j in range(2, 40) if 2**j < devices * blocks and 2**j // blocks > 2}
    )
    shards = {1: shifted(own, 1)}
    for offset in reversed(far_offsets):
        if offset == inner and 2 * offset in shards:
            odd = device // inner % 2 == 1
            give = jnp.where(odd, shards[2 * offset], own)
            shards[offset] = move(give, [(i, i ^ inner) for i in range(devices)])
        else:
            shards[offset] = shifted(own, offset)
    shards[2] = shifted(shards[1], 1)

    def phase(near, far, carry, last, name):
        return attend(
            block_lists,
            query_matrix,
            {o: shards[o] if o else own for o in near},
            {o: shards[o] for o in far},
            carry,
            last,
            name,
        )

    carry = phase([0], [], None, False, "own")
    carry = phase([1], [], carry, False, "one")
    carry = phase([], far_offsets, carry, False, "far")
    return phase([2], [], carry, True, "two")


def solution(mesh):
    spec = P(("ctxhi", "ctxlo"), None)
    return jax.shard_map(
        body, mesh=mesh, in_specs=(spec,) * 4, out_specs=spec, check_vma=False
    )
```

time: 63.4 us -> 49.6 us (0.78)
  Pallas kernels: 31.9 us -> 18.9 us
  waiting for transfers between devices: 18.5 us -> 17.7 us
    pallas_call x3 -> x4, Pallas kernels: 31.9 us -> 18.9 us  [attend(): pl.pallas_call(functools.partial(attend_kernel, tuple(near), tuple(far),...]
    ppermute x5, waiting for transfers between devices: 18.5 us -> 17.7 us  [move(): lax.ppermute(block, ('ctxlo', 'ctxhi'), [(place(a), place(b)) for a, b in...]
where the time goes in v2:
time: 49.6 us; the launch traced here: 49 us
  Pallas kernels  18.9 us (38%)
  waiting for transfers between devices  17.7 us (36%)
  starting transfers between devices  10.2 us (21%)
  local copies, waits for them, and re-layouts  2.07 us (4%)
    pallas_call x4, Pallas kernels, attend(): pl.pallas_call(functools.partial(attend_kernel, tuple(near), tuple(far),...  18.9 us
    ppermute x5, waiting for transfers between devices, move(): lax.ppermute(block, ('ctxlo', 'ctxhi'), [(place(a), place(b)) for a, b in...  17.7 us
    ppermute x5, starting transfers between devices, move(): lax.ppermute(block, ('ctxlo', 'ctxhi'), [(place(a), place(b)) for a, b in...  10.2 us
    unnamed x5, local copies, waits for them, and re-layouts  1.1 us
  transfers between devices with their start and end apart: 5, of which 3 were waited for; matrix products, arithmetic and copies ran while one was open for 0% of the time, Pallas kernels for 29%

profile of v2, /device:TPU:4, one launch (start us, length us, event | category | flops | bytes accessed | tf_op | source)
XLA Modules:
  0.0 49.0 jit_solution(711586608716695626)
XLA Ops:
  0.0 0.0 copy-start
  0.0 0.0 copy-start.1
  0.0 1.1 %constant_dynamic-update-slice_fusion.1 = f32[256,512]{1,0:T(8,128)S(1)} fusion(f32[256,256]{1,0:T(8,128)} %param.5), kind=kLoop, calls=%fused_computation.2 | loop fusion | bytes 524288
  1.1 1.0 %constant_dynamic-update-slice_fusion.refs_2_ = f32[256,512]{1,0:T(8,128)S(1)} fusion(f32[256,512]{1,0:T(8,128)S(1)} %constant_dynamic-update-slice_fusion.1, f32[256,256]{1,0:T(8,128)} %param.6), kind=kLoop, calls=%fused_computation.1 | loop fusion | bytes 524288 | tf_op jit(solution)/shard_map/concatenate | solution.py:268
  2.1 3.4 %collective-permute-start.2 = (f32[256,512]{1,0:T(8,128)S(1)}, f32[256,512]{1,0:T(8,128)S(1)}, u32[]{:S(2)}, u32[]{:S(2)}) collective-permute-start(f32[256,512]{1,0:T(8,128)S(1)} %constant_dynamic-update-slice_fusion.refs_2_), channel_id=1, source_target_pairs={{0,2},{8,10},{16,18},{24,26},{1,3},{9,11},{17,19},{25,27},{2,4},{1... | collective-permute-start | bytes 1572872 | tf_op jit(solution)/shard_map/ppermute | solution.py:263
  5.5 3.5 %collective-permute-start = (f32[256,512]{1,0:T(8,128)S(1)}, f32[256,512]{1,0:T(8,128)S(1)}, u32[]{:S(2)}, u32[]{:S(2)}) collective-permute-start(f32[256,512]{1,0:T(8,128)S(1)} %constant_dynamic-update-slice_fusion.refs_2_), channel_id=1, source_target_pairs={{0,8},{8,16},{16,24},{24,1},{1,9},{9,17},{17,25},{25,2},{2,10},{10... | collective-permute-start | bytes 1572872 | tf_op jit(solution)/shard_map/ppermute | solution.py:263
  9.0 1.3 %collective-permute-start.4 = (f32[256,512]{1,0:T(8,128)S(1)}, f32[256,512]{1,0:T(8,128)}, u32[]{:S(2)}, u32[]{:S(2)}) collective-permute-start(f32[256,512]{1,0:T(8,128)S(1)} %constant_dynamic-update-slice_fusion.refs_2_), channel_id=1, source_target_pairs={{0,4},{8,12},{16,20},{24,28},{1,5},{9,13},{17,21},{25,29},{2,6},{1... | collective-permute-start | bytes 1572872 | tf_op jit(solution)/shard_map/ppermute | solution.py:263
  10.3 12.9 %collective-permute-done.2.refs_3_ = f32[256,512]{1,0:T(8,128)S(1)} collective-permute-done((f32[256,512]{1,0:T(8,128)S(1)}, f32[256,512]{1,0:T(8,128)S(1)}, u32[]{:S(2)}, u32[]{:S(2)}) %collective-permute-start.2) | collective-permute-done | bytes 524320 | tf_op jit(solution)/shard_map/ppermute | solution.py:263
  23.3 0.1 broadcast_select_fusion
  23.3 0.1 collective-permute-start.3
  23.4 1.2 %collective-permute-done.refs_2_ = f32[256,512]{1,0:T(8,128)S(1)} collective-permute-done((f32[256,512]{1,0:T(8,128)S(1)}, f32[256,512]{1,0:T(8,128)S(1)}, u32[]{:S(2)}, u32[]{:S(2)}) %collective-permute-start) | collective-permute-done | bytes 524320 | tf_op jit(solution)/shard_map/ppermute | solution.py:263
  24.7 1.9 %collective-permute-start.1 = (f32[256,512]{1,0:T(8,128)S(1)}, f32[256,512]{1,0:T(8,128)S(1)}, u32[]{:S(2)}, u32[]{:S(2)}) collective-permute-start(f32[256,512]{1,0:T(8,128)S(1)} %collective-permute-done.refs_2_), channel_id=1, source_target_pairs={{0,8},{8,16},{16,24},{24,1},{1,9},{9,17},{17,25},{25,2},{2,10},{10... | collective-permute-start | bytes 1572872 | tf_op jit(solution)/shard_map/ppermute | solution.py:263
  26.6 0.0 copy-done
  26.6 0.0 copy-done.1
  26.6 3.7 %own.1 = (f32[256,1536]{1,0:T(8,128)S(1)}, f32[3072,128]{1,0:T(8,128)S(1)}, f32[3072,128]{1,0:T(8,128)S(1)}) custom-call(s32[2,15]{1,0:T(2,128)S(1)} %copy-done.1, f32[256,1536]{1,0:T(8,128)S(1)} %copy-done, f32[256,512]{1,0:T(8,128)S(1)} %constant_dynamic-update-slice_fusion.refs_2_), custom_call_target="tpu_custom_call" | custom-call | flops 1610612736 | bytes 6291456 | tf_op jit(solution)/shard_map/own/pallas_call | solution.py:236
  30.2 4.0 %one.1 = (f32[256,1536]{1,0:T(8,128)S(1)}, f32[3072,128]{1,0:T(8,128)S(1)}, f32[3072,128]{1,0:T(8,128)S(1)}) custom-call(s32[2,15]{1,0:T(2,128)S(1)} %copy-done.1, f32[256,1536]{1,0:T(8,128)S(1)} %copy-done, f32[256,512]{1,0:T(8,128)S(1)} %collective-permute-done.refs_2_, f32[256,1536]{1,0:T(8,128)S(1)} %get-tuple-element.14.refs_3_, ...), custom_call_target="tpu_custom_call" | custom-call | flops 1610612736 | bytes 6291456 | tf_op jit(solution)/shard_map/one/pallas_call | solution.py:236
  34.3 3.5 %collective-permute-done.4.refs_4_ = f32[256,512]{1,0:T(8,128)} collective-permute-done((f32[256,512]{1,0:T(8,128)S(1)}, f32[256,512]{1,0:T(8,128)}, u32[]{:S(2)}, u32[]{:S(2)}) %collective-permute-start.4) | collective-permute-done | bytes 524320 | tf_op jit(solution)/shard_map/ppermute | solution.py:263
  37.8 0.0 collective-permute-done.3.refs_2_
  37.8 6.5 %far.1 = (f32[256,1536]{1,0:T(8,128)S(1)}, f32[3072,128]{1,0:T(8,128)S(1)}, f32[3072,128]{1,0:T(8,128)S(1)}) custom-call(s32[2,15]{1,0:T(2,128)S(1)} %copy-done.1, f32[256,1536]{1,0:T(8,128)S(1)} %copy-done, f32[256,512]{1,0:T(8,128)S(1)} %collective-permute-done.3.refs_2_, f32[256,512]{1,0:T(8,128)S(1)} %collective-permute-done.2.refs_3_, ...), custom_call_target="tpu_custom_call" | custom-call | flops 2415919104 | bytes 6291456 | tf_op jit(solution)/shard_map/far/pallas_call | solution.py:236
  44.3 0.0 collective-permute-done.1.refs_2_
  44.3 4.7 %two.1 = f32[256,1536]{1,0:T(8,128)} custom-call(s32[2,15]{1,0:T(2,128)S(1)} %copy-done.1, f32[256,1536]{1,0:T(8,128)S(1)} %copy-done, f32[256,512]{1,0:T(8,128)S(1)} %collective-permute-done.1.refs_2_, f32[256,1536]{1,0:T(8,128)S(1)} %get-tuple-element.20.refs_3_, f32[3072,128]{1,0:T(8,128)S(1)} %get-tuple-element.21.refs_4_, ...), custom_call_target="tpu_custom_call" | custom-call | flops 1610612736 | bytes 6291456 | tf_op jit(solution)/shard_map/two/pallas_call | solution.py:236
Async XLA Ops:
  0.0 26.6 %copy-start = (f32[256,1536]{1,0:T(8,128)S(1)}, f32[256,1536]{1,0:T(8,128)}, u32[]{:S(2)}) copy-start(f32[256,1536]{1,0:T(8,128)} %refs_1_.7) | copy-start | bytes 4718596
  0.0 26.6 %copy-start.1 = (s32[2,15]{1,0:T(2,128)S(1)}, s32[2,15]{1,0:T(2,128)}, u32[]{:S(2)}) copy-start(s32[2,15]{1,0:T(2,128)} %refs_0_.7) | copy-start | bytes 364
  2.1 21.2 %collective-permute-start.2 = (f32[256,512]{1,0:T(8,128)S(1)}, f32[256,512]{1,0:T(8,128)S(1)}, u32[]{:S(2)}, u32[]{:S(2)}) collective-permute-start(f32[256,512]{1,0:T(8,128)S(1)} %constant_dynamic-update-slice_fusion.refs_2_), channel_id=1, source_target_pairs={{0,2},{8,10},{16,18},{24,26},{1,3},{9,11},{17,19},{25,27},{2,4},{1... | collective-permute-start | bytes 1572872 | tf_op jit(solution)/shard_map/ppermute | solution.py:263
  5.5 19.2 %collective-permute-start = (f32[256,512]{1,0:T(8,128)S(1)}, f32[256,512]{1,0:T(8,128)S(1)}, u32[]{:S(2)}, u32[]{:S(2)}) collective-permute-start(f32[256,512]{1,0:T(8,128)S(1)} %constant_dynamic-update-slice_fusion.refs_2_), channel_id=1, source_target_pairs={{0,8},{8,16},{16,24},{24,1},{1,9},{9,17},{17,25},{25,2},{2,10},{10... | collective-permute-start | bytes 1572872 | tf_op jit(solution)/shard_map/ppermute | solution.py:263
  9.0 28.8 %collective-permute-start.4 = (f32[256,512]{1,0:T(8,128)S(1)}, f32[256,512]{1,0:T(8,128)}, u32[]{:S(2)}, u32[]{:S(2)}) collective-permute-start(f32[256,512]{1,0:T(8,128)S(1)} %constant_dynamic-update-slice_fusion.refs_2_), channel_id=1, source_target_pairs={{0,4},{8,12},{16,20},{24,28},{1,5},{9,13},{17,21},{25,29},{2,6},{1... | collective-permute-start | bytes 1572872 | tf_op jit(solution)/shard_map/ppermute | solution.py:263
  23.3 14.4 %collective-permute-start.3 = (f32[256,512]{1,0:T(8,128)S(1)}, f32[256,512]{1,0:T(8,128)S(1)}, u32[]{:S(2)}, u32[]{:S(2)}) collective-permute-start(f32[256,512]{1,0:T(8,128)S(1)} %broadcast_select_fusion), channel_id=1, source_target_pairs={{0,1},{8,9},{16,17},{24,25},{1,0},{9,8},{17,16},{25,24},{2,3},{10,... | collective-permute-start | bytes 1572872 | tf_op jit(solution)/shard_map/ppermute | solution.py:263
  24.7 19.6 %collective-permute-start.1 = (f32[256,512]{1,0:T(8,128)S(1)}, f32[256,512]{1,0:T(8,128)S(1)}, u32[]{:S(2)}, u32[]{:S(2)}) collective-permute-start(f32[256,512]{1,0:T(8,128)S(1)} %collective-permute-done.refs_2_), channel_id=1, source_target_pairs={{0,8},{8,16},{16,24},{24,1},{1,9},{9,17},{17,25},{25,2},{2,10},{10... | collective-permute-start | bytes 1572872 | tf_op jit(solution)/shard_map/ppermute | solution.py:263

commit v3 on v2

--- a/solution.py
+++ b/solution.py
@@ -7,6 +7,7 @@
 from jax.experimental import pallas as pl
 from jax.experimental.pallas import tpu as pltpu
 from jax.sharding import PartitionSpec as P
+
 
 QUERY_HEADS = 12
 KEY_VALUE_HEADS = 2
@@ -28,7 +29,8 @@
     refs = list(refs)
     lists_ref, q_ref = refs.pop(0), refs.pop(0)
     near_refs = [refs.pop(0) for _ in near]
-    far_refs = [refs.pop(0) for _ in far]
+    far_refs = [[refs.pop(0) for _ in range(pieces)] for _, pieces in far]
+    far = [offset for offset, _ in far]
     if not first:
         acc_in, peak_in, total_in = refs.pop(0), refs.pop(0), refs.pop(0)
     if last:
@@ -54,22 +56,31 @@
     device = lax.axis_index("ctxhi") * lax.axis_size("ctxlo") + lax.axis_index("ctxlo")
     near_keys = len(near) * tokens
     keys = near_keys + len(far) * BLOCK_TOKENS
-
-    def prepare(kv, g, k_terms, v_terms, index, at):
-        rows = kv.shape[0]
-        high, low = split(kv[:, g * HEAD_FEATURES : (g + 1) * HEAD_FEATURES])
-        k_terms[index, at : at + rows, :] = jnp.concatenate([high, high, low], axis=1)
-        v = groups + g
-        terms = jnp.concatenate(split(kv[:, v * HEAD_FEATURES : (v + 1) * HEAD_FEATURES]), axis=1)
-        v_terms[index, 2 * at : 2 * at + rows, :] = terms
-        v_terms[index, 2 * at + rows : 2 * (at + rows), :] = terms
+    single = keys == BLOCK_TOKENS
+
+    def prepare(pieces, g, k_terms, v_terms, index, at):
+        rows = pieces[0].shape[0]
+
+        def part(n):
+            cols = slice(n * HEAD_FEATURES, (n + 1) * HEAD_FEATURES)
+            return functools.reduce(jnp.add, [piece[:, cols] for piece in pieces])
+
+        high, low = split(part(g))
+        terms = jnp.concatenate(split(part(groups + g)), axis=1)
+        v_terms[index, at : at + rows, :] = terms
+        if single:
+            k_terms[index, :rows, :] = jnp.concatenate([high, high], axis=1)
+            k_terms[index, rows:, :] = jnp.concatenate([low, low], axis=1)
+            v_terms[index, rows:, :] = terms
+        else:
+            k_terms[index, at : at + rows, :] = jnp.concatenate([high, high, low], axis=1)
 
     for g in range(groups):
         for n, ref in enumerate(near_refs):
-            prepare(ref, g, k_near, v_near, g, n * tokens)
+            prepare([ref], g, k_near, v_near, g, n * tokens)
         for b in range(blocks):
-            for n, ref in enumerate(far_refs):
-                block = ref.at[b * BLOCK_TOKENS : (b + 1) * BLOCK_TOKENS]
+            for n, pieces in enumerate(far_refs):
+                block = [ref.at[b * BLOCK_TOKENS : (b + 1) * BLOCK_TOKENS] for ref in pieces]
                 prepare(block, g, k_far, v_far, b * groups + g, n * BLOCK_TOKENS)
 
     def place(step, half):
@@ -81,7 +92,7 @@
         return block, group, row, col, stat
 
     def score(step, half):
-        block, group, row, col, _ = place(step, half)
+        _, group, row, col, _ = place(step, half)
         q = jnp.concatenate(
             [
                 q_ref[pl.ds(row, BLOCK_TOKENS), pl.ds(col + h * HEAD_FEATURES, HEAD_FEATURES)]
@@ -90,8 +101,13 @@
             axis=0,
         )
         high, low = split(q * SCALE)
+        dims = (((1,), (1,)), ((), ()))
+        if single:
+            terms = jnp.concatenate([high, low], axis=1)
+            both = lax.dot_general(terms, k_far[step], dims, preferred_element_type=F32)
+            scores[half][...] = both[:, :BLOCK_TOKENS] + both[:, BLOCK_TOKENS:]
+            return
         terms = jnp.concatenate([high, low, high], axis=1)
-        dims = (((1,), (1,)), ((), ()))
         if near:
             scores[half][:, :near_keys] = lax.dot_general(
                 terms, k_near[group], dims, preferred_element_type=F32
@@ -102,7 +118,7 @@
             )
 
     def soften(step, half):
-        block, group, _, _, stat = place(step, half)
+        block, _, _, _, stat = place(step, half)
 
         def bias(key_block):
             hit = lists_ref[block, 0] == key_block
@@ -148,27 +164,25 @@
                 peak_out[at, :] = peak
                 total_out[at, :] = total
             for n, part in enumerate(parts):
-                start = n * BLOCK_TOKENS
-                if start < near_keys:
-                    base, size = start // tokens * tokens, tokens
+                cols = slice(n * BLOCK_TOKENS, (n + 1) * BLOCK_TOKENS)
+                high, low = split(part)
+                weights[half][rows, cols] = high
+                if single:
+                    weights[half][rows, BLOCK_TOKENS:] = low
                 else:
-                    base, size = start, BLOCK_TOKENS
-                high, low = split(part)
-                here = start + base
-                weights[half][rows, here : here + BLOCK_TOKENS] = high
-                weights[half][rows, here + size : here + size + BLOCK_TOKENS] = low
+                    weights[half][CHAIN_ROWS + h * BLOCK_TOKENS : CHAIN_ROWS + (h + 1) * BLOCK_TOKENS, cols] = low
 
     def gather(step, half):
-        block, group, row, col, _ = place(step, half)
+        _, group, row, col, _ = place(step, half)
         both = None
         if near:
-            both = jnp.dot(
-                weights[half][:, : 2 * near_keys], v_near[group], preferred_element_type=F32
-            )
+            both = jnp.dot(weights[half][:, :near_keys], v_near[group], preferred_element_type=F32)
         if far:
-            more = jnp.dot(weights[half][:, 2 * near_keys :], v_far[step], preferred_element_type=F32)
+            more = jnp.dot(weights[half][:, near_keys:], v_far[step], preferred_element_type=F32)
             both = more if both is None else both + more
-        acc = both[:, :HEAD_FEATURES] + both[:, HEAD_FEATURES:]
+        acc = both[:CHAIN_ROWS, :HEAD_FEATURES] + both[:CHAIN_ROWS, HEAD_FEATURES:]
+        if not single:
+            acc = acc + both[CHAIN_ROWS:, :HEAD_FEATURES]
         for h in range(CHAIN_HEADS):
             rows = slice(h * BLOCK_TOKENS, (h + 1) * BLOCK_TOKENS)
             at = (pl.ds(row, BLOCK_TOKENS), pl.ds(col + h * HEAD_FEATURES, HEAD_FEATURES))
@@ -186,21 +200,17 @@
         return pltpu.make_async_copy(acc_out.at[at], out_hbm.at[at], out_sem.at[step])
 
     score(0, 0)
-
-    @pl.loop(0, steps)
-    def _(step):
+    for step in range(steps):
         score(step, 1)
         soften(step, 0)
-        gather(jnp.maximum(step - 1, 0), 1)
-        score(jnp.minimum(step + 1, steps - 1), 0)
+        if step:
+            gather(step - 1, 1)
+            if last:
+                send(step - 1).start()
+        if step + 1 < steps:
+            score(step + 1, 0)
         soften(step, 1)
         gather(step, 0)
-        if last:
-
-            @pl.when(step > 0)
-            def _():
-                send(step - 1).start()
-
     gather(steps - 1, 1)
     if last:
         send(steps - 1).start()
@@ -208,33 +218,37 @@
             send(step).wait()
 
 
-def attend(lists, query, near, far, carry, last, name):
+def attend(lists, query, near, far, carry, last):
     tokens, width = query.shape
     blocks = tokens // BLOCK_TOKENS
     steps = blocks * KEY_VALUE_HEADS
     first = carry is None
     vmem = pl.BlockSpec(memory_space=pltpu.VMEM)
-    operands = [lists, query, *near.values(), *far.values()] + ([] if first else list(carry))
+    operands = [lists, query, *near.values(), *sum(far.values(), ())] + ([] if first else list(carry))
     specs = [pl.BlockSpec(memory_space=pltpu.SMEM)] + [vmem] * (len(operands) - 1)
     wide = jax.ShapeDtypeStruct((tokens, width), F32)
-    stat = jax.ShapeDtypeStruct((tokens * QUERY_HEADS, BLOCK_TOKENS), F32)
+    stat = pltpu.VMEM((tokens * QUERY_HEADS, BLOCK_TOKENS), F32)
     near_keys, far_keys = len(near) * tokens, len(far) * BLOCK_TOKENS
     keys = near_keys + far_keys
     scratch = [pltpu.VMEM((CHAIN_ROWS, keys), F32)] * 2
-    scratch += [pltpu.VMEM((CHAIN_ROWS, 2 * keys), BF16)] * 2
+    single = keys == BLOCK_TOKENS
+    shape = (CHAIN_ROWS, 2 * keys) if single else (2 * CHAIN_ROWS, keys)
+    scratch += [pltpu.VMEM(shape, BF16)] * 2
     scratch += [pltpu.VMEM((CHAIN_ROWS, 2 * BLOCK_TOKENS), F32)] * 2
     for number, size in ((KEY_VALUE_HEADS, near_keys), (steps, far_keys)):
         if size:
-            scratch.append(pltpu.VMEM((number, size, 3 * HEAD_FEATURES), BF16))
-            scratch.append(pltpu.VMEM((number, 2 * size, 2 * HEAD_FEATURES), BF16))
+            terms, size = (2, 2 * size) if single else (3, size)
+            scratch.append(pltpu.VMEM((number, size, terms * HEAD_FEATURES), BF16))
+            scratch.append(pltpu.VMEM((number, size, 2 * HEAD_FEATURES), BF16))
     if last:
         scratch += [pltpu.VMEM((tokens, width), F32), pltpu.SemaphoreType.DMA((steps,))]
         out_shape, out_specs = wide, pl.BlockSpec(memory_space=pl.ANY)
     else:
-        out_shape, out_specs = (wide, stat, stat), (vmem,) * 3
+        out_shape, out_specs = (pltpu.VMEM((tokens, width), F32), stat, stat), (vmem,) * 3
     pairs = tokens * QUERY_HEADS * keys
+    pieces = tuple((offset, len(arrays)) for offset, arrays in far.items())
     return pl.pallas_call(
-        functools.partial(attend_kernel, tuple(near), tuple(far), first, last),
+        functools.partial(attend_kernel, tuple(near), pieces, first, last),
         in_specs=specs,
         out_specs=out_specs,
         out_shape=out_shape,
@@ -243,18 +257,43 @@
         cost_estimate=pl.CostEstimate(
             flops=pairs * HEAD_FEATURES * 16, bytes_accessed=4 * tokens * width * 4, transcendentals=pairs
         ),
-        name=name,
     )(*operands)
 
 
-VMEM_LIMIT = 40 * 2**20
+VMEM_LIMIT = 20 * 2**20
+
+
+def pack_kernel(k_ref, v_ref, out_ref, sems):
+    width = k_ref.shape[1]
+    copies = [
+        pltpu.make_async_copy(ref, out_ref.at[:, n * width : (n + 1) * width], sems.at[n])
+        for n, ref in enumerate((k_ref, v_ref))
+    ]
+    for copy in copies:
+        copy.start()
+    for copy in copies:
+        copy.wait()
+
+
+def pack(keys, values):
+    rows, width = keys.shape
+    hbm = pl.BlockSpec(memory_space=pltpu.HBM)
+    return pl.pallas_call(
+        pack_kernel,
+        in_specs=[hbm, hbm],
+        out_specs=pl.BlockSpec(memory_space=pltpu.VMEM),
+        out_shape=jax.ShapeDtypeStruct((rows, 2 * width), F32),
+        scratch_shapes=[pltpu.SemaphoreType.DMA((2,))],
+        compiler_params=pltpu.CompilerParams(vmem_limit_bytes=2 * 2**20),
+        name="pack",
+    )(keys, values)
+
 
 def body(query_matrix, key_matrix, value_matrix, block_lists):
     blocks = query_matrix.shape[0] // BLOCK_TOKENS
     inner = lax.axis_size("ctxlo")
     outer = lax.axis_size("ctxhi")
     devices = inner * outer
-    device = lax.axis_index("ctxhi") * inner + lax.axis_index("ctxlo")
 
     def place(shard):
         return shard % inner * outer + shard // inner
@@ -265,39 +304,45 @@
     def shifted(block, offset):
         return move(block, [(i, i + offset) for i in range(devices - offset)])
 
-    own = jnp.concatenate([key_matrix, value_matrix], axis=1)
+    own = pack(key_matrix, value_matrix)
     far_offsets = sorted(
         {2**j // blocks for j in range(2, 40) if 2**j < devices * blocks and 2**j // blocks > 2}
     )
-    shards = {1: shifted(own, 1)}
-    for offset in reversed(far_offsets):
-        if offset == inner and 2 * offset in shards:
-            odd = device // inner % 2 == 1
-            give = jnp.where(odd, shards[2 * offset], own)
-            shards[offset] = move(give, [(i, i ^ inner) for i in range(devices)])
-        else:
-            shards[offset] = shifted(own, offset)
+    pair = 2 * inner
+    shards = {0: own, 1: shifted(own, 1)}
     shards[2] = shifted(shards[1], 1)
-
-    def phase(near, far, carry, last, name):
+    far = {}
+    for offset in far_offsets:
+        if offset != inner or pair not in far_offsets:
+            far[offset] = (shifted(own, offset),)
+    if inner not in far:
+        odd = [i for i in range(devices) if i // inner % 2]
+        far[inner] = (
+            move(own, [(i - inner, i) for i in odd]),
+            move(far[pair][0], [(i, i - inner) for i in odd]),
+        )
+
+    def phase(near_offsets, far_offsets, carry, last):
         return attend(
             block_lists,
             query_matrix,
-            {o: shards[o] if o else own for o in near},
-            {o: shards[o] for o in far},
+            {o: shards[o] for o in near_offsets},
+            {o: far[o] for o in far_offsets},
             carry,
             last,
-            name,
         )
 
-    carry = phase([0], [], None, False, "own")
-    carry = phase([1], [], carry, False, "one")
-    carry = phase([], far_offsets, carry, False, "far")
-    return phase([2], [], carry, True, "two")
+    soon = [o for o in (inner, pair) if o in far]
+    rest = [o for o in far if o not in soon]
+    carry = phase([0], [], None, False)
+    carry = phase([1], [], carry, False)
+    carry = phase([], soon, carry, False)
+    carry = phase([2], [], carry, not rest)
+    if rest:
+        carry = phase([], rest, carry, True)
+    return carry if isinstance(carry, jax.Array) else carry[0]
 
 
 def solution(mesh):
     spec = P(("ctxhi", "ctxlo"), None)
-    return jax.shard_map(
-        body, mesh=mesh, in_specs=(spec,) * 4, out_specs=spec, check_vma=False
-    )
+    return jax.shard_map(body, mesh=mesh, in_specs=(spec,) * 4, out_specs=spec, check_vma=False)

time: 49.6 us -> 53 us (1.069)
  Pallas kernels: 18.9 us -> 16.1 us
  starting transfers between devices: 10.2 us -> 12.7 us
  local copies, waits for them, and re-layouts: 2.07 us -> 3.98 us
  waiting for transfers between devices: 17.7 us -> 19.2 us
    unnamed x5 -> x10, local copies, waits for them, and re-layouts: 1.1 us -> 3.98 us
    pallas_call x4 -> x6, Pallas kernels: 18.9 us -> 16.1 us  [the longest x5 16.1 us: attend(): pl.pallas_call(functools.partial(attend_kernel, tuple(near), pieces, firs...]
    ppermute x5 -> x6, starting transfers between devices: 10.2 us -> 12.7 us  [move(): lax.ppermute(block, ('ctxlo', 'ctxhi'), [(place(a), place(b)) for a, b in...]
    ppermute x5 -> x6, waiting for transfers between devices: 17.7 us -> 19.2 us  [move(): lax.ppermute(block, ('ctxlo', 'ctxhi'), [(place(a), place(b)) for a, b in...]
    concatenate x1 -> x0, local copies, waits for them, and re-layouts: 0.98 us -> none  [body(): own = jnp.concatenate([key_matrix, value_matrix], axis=1)]
  transfers between devices with their start and end apart: 5 -> 6, of which waited for: 3 -> 4; matrix products, arithmetic and copies ran while one was open for 0% -> 0% of each run, Pallas kernels for 29% -> 24%
where the time goes in v3:
time: 53 us; the launch traced here: 52.1 us
  waiting for transfers between devices  19.2 us (36%)
  Pallas kernels  16.1 us (30%)
  starting transfers between devices  12.7 us (24%)
  local copies, waits for them, and re-layouts  3.98 us (8%)
    ppermute x6, waiting for transfers between devices, move(): lax.ppermute(block, ('ctxlo', 'ctxhi'), [(place(a), place(b)) for a, b in...  19.2 us
    pallas_call x5, Pallas kernels, attend(): pl.pallas_call(functools.partial(attend_kernel, tuple(near), pieces, firs...  16.1 us
    ppermute x6, starting transfers between devices, move(): lax.ppermute(block, ('ctxlo', 'ctxhi'), [(place(a), place(b)) for a, b in...  12.7 us
    unnamed x10, local copies, waits for them, and re-layouts  3.98 us
  transfers between devices with their start and end apart: 6, of which 4 were waited for; matrix products, arithmetic and copies ran while one was open for 0% of the time, Pallas kernels for 24%

profile of v3, /device:TPU:4, one launch (start us, length us, event | category | flops | bytes accessed | tf_op | source)
XLA Modules:
  0.0 52.1 jit_solution(6999027705998870246)
XLA Ops:
  0.0 0.9 %copy-done.2 = f32[256,256]{1,0:T(8,128)S(1)} copy-done((f32[256,256]{1,0:T(8,128)S(1)}, f32[256,256]{1,0:T(8,128)}, u32[]{:S(2)}) %copy-start.2) | copy-done | bytes 262168
  1.0 0.9 %copy-done.3 = f32[256,256]{1,0:T(8,128)S(1)} copy-done((f32[256,256]{1,0:T(8,128)S(1)}, f32[256,256]{1,0:T(8,128)}, u32[]{:S(2)}) %copy-start.3) | copy-done | bytes 262168
  1.9 0.1 pack.1.refs_2_
  2.0 3.4 %collective-permute-start.4 = (f32[256,512]{1,0:T(8,128)S(1)}, f32[256,512]{1,0:T(8,128)S(1)}, u32[]{:S(2)}, u32[]{:S(2)}) collective-permute-start(f32[256,512]{1,0:T(8,128)S(1)} %pack.1.refs_2_), channel_id=1, source_target_pairs={{0,2},{8,10},{16,18},{24,26},{1,3},{9,11},{17,19},{25,27},{2,4},{1... | collective-permute-start | bytes 1572872 | tf_op jit(solution)/shard_map/ppermute | solution.py:302
  5.4 3.5 %collective-permute-start.1 = (f32[256,512]{1,0:T(8,128)S(1)}, f32[256,512]{1,0:T(8,128)S(1)}, u32[]{:S(2)}, u32[]{:S(2)}) collective-permute-start(f32[256,512]{1,0:T(8,128)S(1)} %pack.1.refs_2_), channel_id=1, source_target_pairs={{0,8},{8,16},{16,24},{24,1},{1,9},{9,17},{17,25},{25,2},{2,10},{10... | collective-permute-start | bytes 1572872 | tf_op jit(solution)/shard_map/ppermute | solution.py:302
  8.9 1.3 %collective-permute-start.3 = (f32[256,512]{1,0:T(8,128)S(1)}, f32[256,512]{1,0:T(8,128)S(1)}, u32[]{:S(2)}, u32[]{:S(2)}) collective-permute-start(f32[256,512]{1,0:T(8,128)S(1)} %pack.1.refs_2_), channel_id=1, source_target_pairs={{0,1},{8,9},{16,17},{24,25},{2,3},{10,11},{18,19},{26,27},{4,5},{1... | collective-permute-start | bytes 1572872 | tf_op jit(solution)/shard_map/ppermute | solution.py:302
  10.2 12.8 %collective-permute-done.4.refs_4_ = f32[256,512]{1,0:T(8,128)S(1)} collective-permute-done((f32[256,512]{1,0:T(8,128)S(1)}, f32[256,512]{1,0:T(8,128)S(1)}, u32[]{:S(2)}, u32[]{:S(2)}) %collective-permute-start.4) | collective-permute-done | bytes 524320 | tf_op jit(solution)/shard_map/ppermute | solution.py:302
  23.0 1.3 %collective-permute-start.5 = (f32[256,512]{1,0:T(8,128)S(1)}, f32[256,512]{1,0:T(8,128)S(1)}, u32[]{:S(2)}, u32[]{:S(2)}) collective-permute-start(f32[256,512]{1,0:T(8,128)S(1)} %collective-permute-done.4.refs_4_), channel_id=1, source_target_pairs={{1,0},{9,8},{17,16},{25,24},{3,2},{11,10},{19,18},{27,26},{5,4},{1... | collective-permute-start | bytes 1572872 | tf_op jit(solution)/shard_map/ppermute | solution.py:302
  24.3 0.2 collective-permute-done.1.refs_2_
  24.5 1.9 %collective-permute-start.2 = (f32[256,512]{1,0:T(8,128)S(1)}, f32[256,512]{1,0:T(8,128)S(1)}, u32[]{:S(2)}, u32[]{:S(2)}) collective-permute-start(f32[256,512]{1,0:T(8,128)S(1)} %collective-permute-done.1.refs_2_), channel_id=1, source_target_pairs={{0,8},{8,16},{16,24},{24,1},{1,9},{9,17},{17,25},{25,2},{2,10},{10... | collective-permute-start | bytes 1572872 | tf_op jit(solution)/shard_map/ppermute | solution.py:302
  26.4 1.3 %collective-permute-start = (f32[256,512]{1,0:T(8,128)S(1)}, f32[256,512]{1,0:T(8,128)S(1)}, u32[]{:S(2)}, u32[]{:S(2)}) collective-permute-start(f32[256,512]{1,0:T(8,128)S(1)} %pack.1.refs_2_), channel_id=1, source_target_pairs={{0,4},{8,12},{16,20},{24,28},{1,5},{9,13},{17,21},{25,29},{2,6},{1... | collective-permute-start | bytes 1572872 | tf_op jit(solution)/shard_map/ppermute | solution.py:302
  27.7 0.0 copy-start
  27.8 1.4 %copy-done = f32[256,1536]{1,0:T(8,128)S(1)} copy-done((f32[256,1536]{1,0:T(8,128)S(1)}, f32[256,1536]{1,0:T(8,128)}, u32[]{:S(2)}) %copy-start) | copy-done | bytes 1572888
  29.2 0.7 %copy-done.4 = s32[2,15]{1,0:T(2,128)S(1)} copy-done((s32[2,15]{1,0:T(2,128)S(1)}, s32[2,15]{1,0:T(2,128)}, u32[]{:S(2)}) %copy-start.4) | copy-done | bytes 144
  29.8 2.9 %shard_map.46 = (f32[256,1536]{1,0:T(8,128)S(1)}, f32[3072,128]{1,0:T(8,128)S(1)}, f32[3072,128]{1,0:T(8,128)S(1)}) custom-call(s32[2,15]{1,0:T(2,128)S(1)} %copy-done.4, f32[256,1536]{1,0:T(8,128)S(1)} %copy-done, f32[256,512]{1,0:T(8,128)S(1)} %pack.1.refs_2_), custom_call_target="tpu_custom_call" | custom-call | flops 1610612736 | bytes 6291456 | tf_op jit(solution)/shard_map/pallas_call | solution.py:250
  32.7 0.0 copy-done.1
  32.8 3.2 %shard_map.47 = (f32[256,1536]{1,0:T(8,128)S(1)}, f32[3072,128]{1,0:T(8,128)S(1)}, f32[3072,128]{1,0:T(8,128)S(1)}) custom-call(s32[2,15]{1,0:T(2,128)S(1)} %copy-done.4, f32[256,1536]{1,0:T(8,128)S(1)} %copy-done.1, f32[256,512]{1,0:T(8,128)S(1)} %collective-permute-done.1.refs_2_, f32[256,1536]{1,0:T(8,128)S(1)} %get-tuple-element.17.refs_3_, ...), custom_call_target="tpu_custom_call" | custom-call | flops 1610612736 | bytes 6291456 | tf_op jit(solution)/shard_map/pallas_call | solution.py:250
  36.0 0.0 collective-permute-done.3.refs_2_
  36.0 0.0 collective-permute-done.5.refs_3_
  36.0 3.3 %shard_map.48 = (f32[256,1536]{1,0:T(8,128)S(1)}, f32[3072,128]{1,0:T(8,128)S(1)}, f32[3072,128]{1,0:T(8,128)S(1)}) custom-call(s32[2,15]{1,0:T(2,128)S(1)} %copy-done.4, f32[256,1536]{1,0:T(8,128)S(1)} %copy-done.1, f32[256,512]{1,0:T(8,128)S(1)} %collective-permute-done.3.refs_2_, f32[256,512]{1,0:T(8,128)S(1)} %collective-permute-done.5.refs_3_, ...), custom_call_target="tpu_custom_call" | custom-call | flops 1610612736 | bytes 6291456 | tf_op jit(solution)/shard_map/pallas_call | solution.py:250
  39.3 4.3 %collective-permute-done.2.refs_2_ = f32[256,512]{1,0:T(8,128)S(1)} collective-permute-done((f32[256,512]{1,0:T(8,128)S(1)}, f32[256,512]{1,0:T(8,128)S(1)}, u32[]{:S(2)}, u32[]{:S(2)}) %collective-permute-start.2) | collective-permute-done | bytes 524320 | tf_op jit(solution)/shard_map/ppermute | solution.py:302
  43.6 3.2 %shard_map.49 = (f32[256,1536]{1,0:T(8,128)S(1)}, f32[3072,128]{1,0:T(8,128)S(1)}, f32[3072,128]{1,0:T(8,128)S(1)}) custom-call(s32[2,15]{1,0:T(2,128)S(1)} %copy-done.4, f32[256,1536]{1,0:T(8,128)S(1)} %copy-done.1, f32[256,512]{1,0:T(8,128)S(1)} %collective-permute-done.2.refs_2_, f32[256,1536]{1,0:T(8,128)S(1)} %get-tuple-element.23.refs_3_, ...), custom_call_target="tpu_custom_call" | custom-call | flops 1610612736 | bytes 6291456 | tf_op jit(solution)/shard_map/pallas_call | solution.py:250
  46.8 1.9 %collective-permute-done.refs_2_ = f32[256,512]{1,0:T(8,128)S(1)} collective-permute-done((f32[256,512]{1,0:T(8,128)S(1)}, f32[256,512]{1,0:T(8,128)S(1)}, u32[]{:S(2)}, u32[]{:S(2)}) %collective-permute-start) | collective-permute-done | bytes 524320 | tf_op jit(solution)/shard_map/ppermute | solution.py:302
  48.7 3.4 %shard_map.50 = f32[256,1536]{1,0:T(8,128)} custom-call(s32[2,15]{1,0:T(2,128)S(1)} %copy-done.4, f32[256,1536]{1,0:T(8,128)S(1)} %copy-done.1, f32[256,512]{1,0:T(8,128)S(1)} %collective-permute-done.refs_2_, f32[256,1536]{1,0:T(8,128)S(1)} %get-tuple-element.26.refs_3_, f32[3072,128]{1,0:T(8,128)S(1)} %get-tuple-element.27.refs_4_, ...), custom_call_target="tpu_custom_call" | custom-call | flops 805306368 | bytes 6291456 | tf_op jit(solution)/shard_map/pallas_call | solution.py:250
  (4 shorter events, 0.0 us)
Async XLA Ops:
  0.0 0.9 %copy-start.2 = (f32[256,256]{1,0:T(8,128)S(1)}, f32[256,256]{1,0:T(8,128)}, u32[]{:S(2)}) copy-start(f32[256,256]{1,0:T(8,128)} %k_ref.1) | copy-start | bytes 786436
  1.0 0.9 %copy-start.3 = (f32[256,256]{1,0:T(8,128)S(1)}, f32[256,256]{1,0:T(8,128)}, u32[]{:S(2)}) copy-start(f32[256,256]{1,0:T(8,128)} %v_ref.1) | copy-start | bytes 786436
  2.0 21.0 %collective-permute-start.4 = (f32[256,512]{1,0:T(8,128)S(1)}, f32[256,512]{1,0:T(8,128)S(1)}, u32[]{:S(2)}, u32[]{:S(2)}) collective-permute-start(f32[256,512]{1,0:T(8,128)S(1)} %pack.1.refs_2_), channel_id=1, source_target_pairs={{0,2},{8,10},{16,18},{24,26},{1,3},{9,11},{17,19},{25,27},{2,4},{1... | collective-permute-start | bytes 1572872 | tf_op jit(solution)/shard_map/ppermute | solution.py:302
  5.4 19.2 %collective-permute-start.1 = (f32[256,512]{1,0:T(8,128)S(1)}, f32[256,512]{1,0:T(8,128)S(1)}, u32[]{:S(2)}, u32[]{:S(2)}) collective-permute-start(f32[256,512]{1,0:T(8,128)S(1)} %pack.1.refs_2_), channel_id=1, source_target_pairs={{0,8},{8,16},{16,24},{24,1},{1,9},{9,17},{17,25},{25,2},{2,10},{10... | collective-permute-start | bytes 1572872 | tf_op jit(solution)/shard_map/ppermute | solution.py:302
  8.9 27.1 %collective-permute-start.3 = (f32[256,512]{1,0:T(8,128)S(1)}, f32[256,512]{1,0:T(8,128)S(1)}, u32[]{:S(2)}, u32[]{:S(2)}) collective-permute-start(f32[256,512]{1,0:T(8,128)S(1)} %pack.1.refs_2_), channel_id=1, source_target_pairs={{0,1},{8,9},{16,17},{24,25},{2,3},{10,11},{18,19},{26,27},{4,5},{1... | collective-permute-start | bytes 1572872 | tf_op jit(solution)/shard_map/ppermute | solution.py:302
  23.0 13.0 %collective-permute-start.5 = (f32[256,512]{1,0:T(8,128)S(1)}, f32[256,512]{1,0:T(8,128)S(1)}, u32[]{:S(2)}, u32[]{:S(2)}) collective-permute-start(f32[256,512]{1,0:T(8,128)S(1)} %collective-permute-done.4.refs_4_), channel_id=1, source_target_pairs={{1,0},{9,8},{17,16},{25,24},{3,2},{11,10},{19,18},{27,26},{5,4},{1... | collective-permute-start | bytes 1572872 | tf_op jit(solution)/shard_map/ppermute | solution.py:302
  24.5 19.1 %collective-permute-start.2 = (f32[256,512]{1,0:T(8,128)S(1)}, f32[256,512]{1,0:T(8,128)S(1)}, u32[]{:S(2)}, u32[]{:S(2)}) collective-permute-start(f32[256,512]{1,0:T(8,128)S(1)} %collective-permute-done.1.refs_2_), channel_id=1, source_target_pairs={{0,8},{8,16},{16,24},{24,1},{1,9},{9,17},{17,25},{25,2},{2,10},{10... | collective-permute-start | bytes 1572872 | tf_op jit(solution)/shard_map/ppermute | solution.py:302
  26.4 22.3 %collective-permute-start = (f32[256,512]{1,0:T(8,128)S(1)}, f32[256,512]{1,0:T(8,128)S(1)}, u32[]{:S(2)}, u32[]{:S(2)}) collective-permute-start(f32[256,512]{1,0:T(8,128)S(1)} %pack.1.refs_2_), channel_id=1, source_target_pairs={{0,4},{8,12},{16,20},{24,28},{1,5},{9,13},{17,21},{25,29},{2,6},{1... | collective-permute-start | bytes 1572872 | tf_op jit(solution)/shard_map/ppermute | solution.py:302
  27.7 1.4 %copy-start = (f32[256,1536]{1,0:T(8,128)S(1)}, f32[256,1536]{1,0:T(8,128)}, u32[]{:S(2)}) copy-start(f32[256,1536]{1,0:T(8,128)} %refs_1_.9) | copy-start | bytes 4718596
  29.2 0.7 %copy-start.4 = (s32[2,15]{1,0:T(2,128)S(1)}, s32[2,15]{1,0:T(2,128)}, u32[]{:S(2)}) copy-start(s32[2,15]{1,0:T(2,128)} %refs_0_.9) | copy-start | bytes 364
  29.8 2.9 %copy-start.1 = (f32[256,1536]{1,0:T(8,128)S(1)}, f32[256,1536]{1,0:T(8,128)}, u32[]{:S(2)}) copy-start(f32[256,1536]{1,0:T(8,128)} %refs_1_.9) | copy-start | bytes 4718596

commit v4 on v3

--- a/solution.py
+++ b/solution.py
@@ -28,7 +28,8 @@
 def attend_kernel(near, far, first, last, *refs):
     refs = list(refs)
     lists_ref, q_ref = refs.pop(0), refs.pop(0)
-    near_refs = [refs.pop(0) for _ in near]
+    near_refs = [[refs.pop(0) for _ in range(pieces)] for _, pieces in near]
+    near = [offset for offset, _ in near]
     far_refs = [[refs.pop(0) for _ in range(pieces)] for _, pieces in far]
     far = [offset for offset, _ in far]
     if not first:
@@ -76,8 +77,8 @@
             k_terms[index, at : at + rows, :] = jnp.concatenate([high, high, low], axis=1)
 
     for g in range(groups):
-        for n, ref in enumerate(near_refs):
-            prepare([ref], g, k_near, v_near, g, n * tokens)
+        for n, pieces in enumerate(near_refs):
+            prepare(pieces, g, k_near, v_near, g, n * tokens)
         for b in range(blocks):
             for n, pieces in enumerate(far_refs):
                 block = [ref.at[b * BLOCK_TOKENS : (b + 1) * BLOCK_TOKENS] for ref in pieces]
@@ -224,7 +225,7 @@
     steps = blocks * KEY_VALUE_HEADS
     first = carry is None
     vmem = pl.BlockSpec(memory_space=pltpu.VMEM)
-    operands = [lists, query, *near.values(), *sum(far.values(), ())] + ([] if first else list(carry))
+    operands = [lists, query, *sum((*near.values(), *far.values()), ())] + ([] if first else list(carry))
     specs = [pl.BlockSpec(memory_space=pltpu.SMEM)] + [vmem] * (len(operands) - 1)
     wide = jax.ShapeDtypeStruct((tokens, width), F32)
     stat = pltpu.VMEM((tokens * QUERY_HEADS, BLOCK_TOKENS), F32)
@@ -246,9 +247,12 @@
     else:
         out_shape, out_specs = (pltpu.VMEM((tokens, width), F32), stat, stat), (vmem,) * 3
     pairs = tokens * QUERY_HEADS * keys
-    pieces = tuple((offset, len(arrays)) for offset, arrays in far.items())
+
+    def pieces(shards):
+        return tuple((offset, len(arrays)) for offset, arrays in shards.items())
+
     return pl.pallas_call(
-        functools.partial(attend_kernel, tuple(near), pieces, first, last),
+        functools.partial(attend_kernel, pieces(near), pieces(far), first, last),
         in_specs=specs,
         out_specs=out_specs,
         out_shape=out_shape,
@@ -309,18 +313,35 @@
         {2**j // blocks for j in range(2, 40) if 2**j < devices * blocks and 2**j // blocks > 2}
     )
     pair = 2 * inner
-    shards = {0: own, 1: shifted(own, 1)}
-    shards[2] = shifted(shards[1], 1)
-    far = {}
-    for offset in far_offsets:
-        if offset != inner or pair not in far_offsets:
-            far[offset] = (shifted(own, offset),)
-    if inner not in far:
+    shards = {0: (own,), 1: (shifted(own, 1),)}
+    far = {
+        offset: (shifted(own, offset),)
+        for offset in far_offsets
+        if pair not in far_offsets or offset not in (inner, pair)
+    }
+    if pair in far_offsets:
+        routes = [(i, i + pair) for i in range(devices - pair)]
+        far[pair] = tuple(
+            move(own, [r for r in routes if r[0] // inner % 2 == core])
+            for core in (1, 0)
+        )
         odd = [i for i in range(devices) if i // inner % 2]
         far[inner] = (
             move(own, [(i - inner, i) for i in odd]),
             move(far[pair][0], [(i, i - inner) for i in odd]),
         )
+
+    turns = []
+    if pair in far:
+        turns = [
+            ((outer_index + 2) * inner - 2, outer_index * inner)
+            for outer_index in range(2, outer - 1, 2)
+        ]
+    turned = {b for _, b in turns}
+    routes = [(i, i + 1) for i in range(devices - 1) if i + 1 not in turned]
+    shards[2] = (move(shards[1][0], routes),)
+    if turns:
+        shards[2] += (move(far[pair][0], turns),)
 
     def phase(near_offsets, far_offsets, carry, last):
         return attend(

time: 53 us -> 47.9 us (0.904)
  the two profiles are of different devices: /device:TPU:4 before, /device:TPU:0 now
where the time goes in v4:
time: 47.9 us; the launch traced here: 47.6 us
  starting transfers between devices  25.6 us (53%)
  Pallas kernels  16.2 us (34%)
  local copies, waits for them, and re-layouts  3.98 us (8%)
  waiting for transfers between devices  1.62 us (3%)
    ppermute x8, starting transfers between devices, move(): lax.ppermute(block, ('ctxlo', 'ctxhi'), [(place(a), place(b)) for a, b in...  25.6 us
    pallas_call x5, Pallas kernels, attend(): pl.pallas_call(functools.partial(attend_kernel, pieces(near), pieces(far)...  16.2 us
    unnamed x10, local copies, waits for them, and re-layouts  3.98 us
    ppermute x8, waiting for transfers between devices, move(): lax.ppermute(block, ('ctxlo', 'ctxhi'), [(place(a), place(b)) for a, b in...  1.62 us
  transfers between devices with their start and end apart: 8, of which 1 were waited for; matrix products, arithmetic and copies ran while one was open for 0% of the time, Pallas kernels for 27%

profile of v4, /device:TPU:0, one launch (start us, length us, event | category | flops | bytes accessed | tf_op | source)
XLA Modules:
  0.0 47.6 jit_solution(16531757692106877327)
XLA Ops:
  0.0 0.9 %copy-done.2 = f32[256,256]{1,0:T(8,128)S(1)} copy-done((f32[256,256]{1,0:T(8,128)S(1)}, f32[256,256]{1,0:T(8,128)}, u32[]{:S(2)}) %copy-start.2) | copy-done | bytes 262168
  1.0 0.9 %copy-done.3 = f32[256,256]{1,0:T(8,128)S(1)} copy-done((f32[256,256]{1,0:T(8,128)S(1)}, f32[256,256]{1,0:T(8,128)}, u32[]{:S(2)}) %copy-start.3) | copy-done | bytes 262168
  1.9 0.1 pack.1.refs_2_
  2.0 0.7 %collective-permute-start.3 = (f32[256,512]{1,0:T(8,128)S(1)}, f32[256,512]{1,0:T(8,128)S(1)}, u32[]{:S(2)}, u32[]{:S(2)}) collective-permute-start(f32[256,512]{1,0:T(8,128)S(1)} %pack.1.refs_2_), channel_id=1, source_target_pairs={{1,3},{9,11},{17,19},{25,27},{3,5},{11,13},{19,21},{27,29},{5,7},{... | collective-permute-start | bytes 1572872 | tf_op jit(solution)/shard_map/ppermute | solution.py:306
  2.7 5.0 %collective-permute-start.1 = (f32[256,512]{1,0:T(8,128)S(1)}, f32[256,512]{1,0:T(8,128)S(1)}, u32[]{:S(2)}, u32[]{:S(2)}) collective-permute-start(f32[256,512]{1,0:T(8,128)S(1)} %pack.1.refs_2_), channel_id=1, source_target_pairs={{0,8},{8,16},{16,24},{24,1},{1,9},{9,17},{17,25},{25,2},{2,10},{10... | collective-permute-start | bytes 1572872 | tf_op jit(solution)/shard_map/ppermute | solution.py:306
  7.7 3.9 %collective-permute-start.5 = (f32[256,512]{1,0:T(8,128)S(1)}, f32[256,512]{1,0:T(8,128)S(1)}, u32[]{:S(2)}, u32[]{:S(2)}) collective-permute-start(f32[256,512]{1,0:T(8,128)S(1)} %pack.1.refs_2_), channel_id=1, source_target_pairs={{0,1},{8,9},{16,17},{24,25},{2,3},{10,11},{18,19},{26,27},{4,5},{1... | collective-permute-start | bytes 1572872 | tf_op jit(solution)/shard_map/ppermute | solution.py:306
  11.6 3.4 %collective-permute-start.7 = (f32[256,512]{1,0:T(8,128)S(1)}, f32[256,512]{1,0:T(8,128)S(1)}, u32[]{:S(2)}, u32[]{:S(2)}) collective-permute-start(f32[256,512]{1,0:T(8,128)S(1)} %pack.1.refs_2_), channel_id=1, source_target_pairs={{0,2},{8,10},{16,18},{24,26},{2,4},{10,12},{18,20},{26,28},{4,6},{... | collective-permute-start | bytes 1572872 | tf_op jit(solution)/shard_map/ppermute | solution.py:306
  15.0 0.0 collective-permute-done.3.refs_4_
  15.0 1.3 %collective-permute-start.6 = (f32[256,512]{1,0:T(8,128)S(1)}, f32[256,512]{1,0:T(8,128)S(1)}, u32[]{:S(2)}, u32[]{:S(2)}) collective-permute-start(f32[256,512]{1,0:T(8,128)S(1)} %collective-permute-done.3.refs_4_), channel_id=1, source_target_pairs={{1,0},{9,8},{17,16},{25,24},{3,2},{11,10},{19,18},{27,26},{5,4},{1... | collective-permute-start | bytes 1572872 | tf_op jit(solution)/shard_map/ppermute | solution.py:306
  16.3 0.7 %collective-permute-start.4 = (f32[256,512]{1,0:T(8,128)S(1)}, f32[256,512]{1,0:T(8,128)S(1)}, u32[]{:S(2)}, u32[]{:S(2)}) collective-permute-start(f32[256,512]{1,0:T(8,128)S(1)} %collective-permute-done.3.refs_4_), channel_id=1, source_target_pairs={{19,2},{21,4},{23,6}} | collective-permute-start | bytes 1572872 | tf_op jit(solution)/shard_map/ppermute | solution.py:306
  17.0 1.6 %collective-permute-done.1.refs_2_ = f32[256,512]{1,0:T(8,128)S(1)} collective-permute-done((f32[256,512]{1,0:T(8,128)S(1)}, f32[256,512]{1,0:T(8,128)S(1)}, u32[]{:S(2)}, u32[]{:S(2)}) %collective-permute-start.1) | collective-permute-done | bytes 524320 | tf_op jit(solution)/shard_map/ppermute | solution.py:306
  18.6 4.4 %collective-permute-start.2 = (f32[256,512]{1,0:T(8,128)S(1)}, f32[256,512]{1,0:T(8,128)S(1)}, u32[]{:S(2)}, u32[]{:S(2)}) collective-permute-start(f32[256,512]{1,0:T(8,128)S(1)} %collective-permute-done.1.refs_2_), channel_id=1, source_target_pairs={{0,8},{8,16},{16,24},{24,1},{1,9},{9,17},{17,25},{2,10},{10,18},{1... | collective-permute-start | bytes 1572872 | tf_op jit(solution)/shard_map/ppermute | solution.py:306
  23.0 6.2 %collective-permute-start = (f32[256,512]{1,0:T(8,128)S(1)}, f32[256,512]{1,0:T(8,128)S(1)}, u32[]{:S(2)}, u32[]{:S(2)}) collective-permute-start(f32[256,512]{1,0:T(8,128)S(1)} %pack.1.refs_2_), channel_id=1, source_target_pairs={{0,4},{8,12},{16,20},{24,28},{1,5},{9,13},{17,21},{25,29},{2,6},{1... | collective-permute-start | bytes 1572872 | tf_op jit(solution)/shard_map/ppermute | solution.py:306
  29.3 0.0 copy-start
  29.3 1.4 %copy-done = f32[256,1536]{1,0:T(8,128)S(1)} copy-done((f32[256,1536]{1,0:T(8,128)S(1)}, f32[256,1536]{1,0:T(8,128)}, u32[]{:S(2)}) %copy-start) | copy-done | bytes 1572888
  30.7 0.7 %copy-done.4 = s32[2,15]{1,0:T(2,128)S(1)} copy-done((s32[2,15]{1,0:T(2,128)S(1)}, s32[2,15]{1,0:T(2,128)}, u32[]{:S(2)}) %copy-start.4) | copy-done | bytes 144
  31.3 2.9 %shard_map.46 = (f32[256,1536]{1,0:T(8,128)S(1)}, f32[3072,128]{1,0:T(8,128)S(1)}, f32[3072,128]{1,0:T(8,128)S(1)}) custom-call(s32[2,15]{1,0:T(2,128)S(1)} %copy-done.4, f32[256,1536]{1,0:T(8,128)S(1)} %copy-done, f32[256,512]{1,0:T(8,128)S(1)} %pack.1.refs_2_), custom_call_target="tpu_custom_call" | custom-call | flops 1610612736 | bytes 6291456 | tf_op jit(solution)/shard_map/pallas_call | solution.py:254
  34.3 3.2 %shard_map.47 = (f32[256,1536]{1,0:T(8,128)S(1)}, f32[3072,128]{1,0:T(8,128)S(1)}, f32[3072,128]{1,0:T(8,128)S(1)}) custom-call(s32[2,15]{1,0:T(2,128)S(1)} %copy-done.4, f32[256,1536]{1,0:T(8,128)S(1)} %copy-done.1, f32[256,512]{1,0:T(8,128)S(1)} %collective-permute-done.1.refs_2_, f32[256,1536]{1,0:T(8,128)S(1)} %get-tuple-element.17.refs_3_, ...), custom_call_target="tpu_custom_call" | custom-call | flops 1610612736 | bytes 6291456 | tf_op jit(solution)/shard_map/pallas_call | solution.py:254
  37.5 0.0 collective-permute-done.7.refs_5_
  37.5 0.0 collective-permute-done.6.refs_3_
  37.5 3.4 %shard_map.48 = (f32[256,1536]{1,0:T(8,128)S(1)}, f32[3072,128]{1,0:T(8,128)S(1)}, f32[3072,128]{1,0:T(8,128)S(1)}) custom-call(s32[2,15]{1,0:T(2,128)S(1)} %copy-done.4, f32[256,1536]{1,0:T(8,128)S(1)} %copy-done.1, f32[256,512]{1,0:T(8,128)S(1)} %collective-permute-done.5.refs_2_, f32[256,512]{1,0:T(8,128)S(1)} %collective-permute-done.6.refs_3_, ...), custom_call_target="tpu_custom_call" | custom-call | flops 1610612736 | bytes 6291456 | tf_op jit(solution)/shard_map/pallas_call | solution.py:254
  40.9 3.2 %shard_map.49 = (f32[256,1536]{1,0:T(8,128)S(1)}, f32[3072,128]{1,0:T(8,128)S(1)}, f32[3072,128]{1,0:T(8,128)S(1)}) custom-call(s32[2,15]{1,0:T(2,128)S(1)} %copy-done.4, f32[256,1536]{1,0:T(8,128)S(1)} %copy-done.1, f32[256,512]{1,0:T(8,128)S(1)} %collective-permute-done.2.refs_2_, f32[256,512]{1,0:T(8,128)S(1)} %collective-permute-done.4.refs_3_, ...), custom_call_target="tpu_custom_call" | custom-call | flops 1610612736 | bytes 6291456 | tf_op jit(solution)/shard_map/pallas_call | solution.py:254
  44.2 0.0 collective-permute-done.refs_2_
  44.2 3.4 %shard_map.50 = f32[256,1536]{1,0:T(8,128)} custom-call(s32[2,15]{1,0:T(2,128)S(1)} %copy-done.4, f32[256,1536]{1,0:T(8,128)S(1)} %copy-done.1, f32[256,512]{1,0:T(8,128)S(1)} %collective-permute-done.refs_2_, f32[256,1536]{1,0:T(8,128)S(1)} %get-tuple-element.26.refs_3_, f32[3072,128]{1,0:T(8,128)S(1)} %get-tuple-element.27.refs_4_, ...), custom_call_target="tpu_custom_call" | custom-call | flops 805306368 | bytes 6291456 | tf_op jit(solution)/shard_map/pallas_call | solution.py:254
  (8 shorter events, 0.0 us)
Async XLA Ops:
  0.0 0.9 %copy-start.2 = (f32[256,256]{1,0:T(8,128)S(1)}, f32[256,256]{1,0:T(8,128)}, u32[]{:S(2)}) copy-start(f32[256,256]{1,0:T(8,128)} %k_ref.1) | copy-start | bytes 786436
  1.0 0.9 %copy-start.3 = (f32[256,256]{1,0:T(8,128)S(1)}, f32[256,256]{1,0:T(8,128)}, u32[]{:S(2)}) copy-start(f32[256,256]{1,0:T(8,128)} %v_ref.1) | copy-start | bytes 786436
  2.0 13.0 %collective-permute-start.3 = (f32[256,512]{1,0:T(8,128)S(1)}, f32[256,512]{1,0:T(8,128)S(1)}, u32[]{:S(2)}, u32[]{:S(2)}) collective-permute-start(f32[256,512]{1,0:T(8,128)S(1)} %pack.1.refs_2_), channel_id=1, source_target_pairs={{1,3},{9,11},{17,19},{25,27},{3,5},{11,13},{19,21},{27,29},{5,7},{... | collective-permute-start | bytes 1572872 | tf_op jit(solution)/shard_map/ppermute | solution.py:306
  2.7 15.9 %collective-permute-start.1 = (f32[256,512]{1,0:T(8,128)S(1)}, f32[256,512]{1,0:T(8,128)S(1)}, u32[]{:S(2)}, u32[]{:S(2)}) collective-permute-start(f32[256,512]{1,0:T(8,128)S(1)} %pack.1.refs_2_), channel_id=1, source_target_pairs={{0,8},{8,16},{16,24},{24,1},{1,9},{9,17},{17,25},{25,2},{2,10},{10... | collective-permute-start | bytes 1572872 | tf_op jit(solution)/shard_map/ppermute | solution.py:306
  7.7 15.4 %collective-permute-start.5 = (f32[256,512]{1,0:T(8,128)S(1)}, f32[256,512]{1,0:T(8,128)S(1)}, u32[]{:S(2)}, u32[]{:S(2)}) collective-permute-start(f32[256,512]{1,0:T(8,128)S(1)} %pack.1.refs_2_), channel_id=1, source_target_pairs={{0,1},{8,9},{16,17},{24,25},{2,3},{10,11},{18,19},{26,27},{4,5},{1... | collective-permute-start | bytes 1572872 | tf_op jit(solution)/shard_map/ppermute | solution.py:306
  11.6 25.9 %collective-permute-start.7 = (f32[256,512]{1,0:T(8,128)S(1)}, f32[256,512]{1,0:T(8,128)S(1)}, u32[]{:S(2)}, u32[]{:S(2)}) collective-permute-start(f32[256,512]{1,0:T(8,128)S(1)} %pack.1.refs_2_), channel_id=1, source_target_pairs={{0,2},{8,10},{16,18},{24,26},{2,4},{10,12},{18,20},{26,28},{4,6},{... | collective-permute-start | bytes 1572872 | tf_op jit(solution)/shard_map/ppermute | solution.py:306
  15.0 22.5 %collective-permute-start.6 = (f32[256,512]{1,0:T(8,128)S(1)}, f32[256,512]{1,0:T(8,128)S(1)}, u32[]{:S(2)}, u32[]{:S(2)}) collective-permute-start(f32[256,512]{1,0:T(8,128)S(1)} %collective-permute-done.3.refs_4_), channel_id=1, source_target_pairs={{1,0},{9,8},{17,16},{25,24},{3,2},{11,10},{19,18},{27,26},{5,4},{1... | collective-permute-start | bytes 1572872 | tf_op jit(solution)/shard_map/ppermute | solution.py:306
  16.3 24.6 %collective-permute-start.4 = (f32[256,512]{1,0:T(8,128)S(1)}, f32[256,512]{1,0:T(8,128)S(1)}, u32[]{:S(2)}, u32[]{:S(2)}) collective-permute-start(f32[256,512]{1,0:T(8,128)S(1)} %collective-permute-done.3.refs_4_), channel_id=1, source_target_pairs={{19,2},{21,4},{23,6}} | collective-permute-start | bytes 1572872 | tf_op jit(solution)/shard_map/ppermute | solution.py:306
  18.6 22.3 %collective-permute-start.2 = (f32[256,512]{1,0:T(8,128)S(1)}, f32[256,512]{1,0:T(8,128)S(1)}, u32[]{:S(2)}, u32[]{:S(2)}) collective-permute-start(f32[256,512]{1,0:T(8,128)S(1)} %collective-permute-done.1.refs_2_), channel_id=1, source_target_pairs={{0,8},{8,16},{16,24},{24,1},{1,9},{9,17},{17,25},{2,10},{10,18},{1... | collective-permute-start | bytes 1572872 | tf_op jit(solution)/shard_map/ppermute | solution.py:306
  23.0 21.1 %collective-permute-start = (f32[256,512]{1,0:T(8,128)S(1)}, f32[256,512]{1,0:T(8,128)S(1)}, u32[]{:S(2)}, u32[]{:S(2)}) collective-permute-start(f32[256,512]{1,0:T(8,128)S(1)} %pack.1.refs_2_), channel_id=1, source_target_pairs={{0,4},{8,12},{16,20},{24,28},{1,5},{9,13},{17,21},{25,29},{2,6},{1... | collective-permute-start | bytes 1572872 | tf_op jit(solution)/shard_map/ppermute | solution.py:306
  29.3 1.4 %copy-start = (f32[256,1536]{1,0:T(8,128)S(1)}, f32[256,1536]{1,0:T(8,128)}, u32[]{:S(2)}) copy-start(f32[256,1536]{1,0:T(8,128)} %refs_1_.9) | copy-start | bytes 4718596
  30.7 0.7 %copy-start.4 = (s32[2,15]{1,0:T(2,128)S(1)}, s32[2,15]{1,0:T(2,128)}, u32[]{:S(2)}) copy-start(s32[2,15]{1,0:T(2,128)} %refs_0_.9) | copy-start | bytes 364
  31.3 2.9 %copy-start.1 = (f32[256,1536]{1,0:T(8,128)S(1)}, f32[256,1536]{1,0:T(8,128)}, u32[]{:S(2)}) copy-start(f32[256,1536]{1,0:T(8,128)} %refs_1_.9) | copy-start | bytes 4718596

commit v5 on v4

--- a/solution.py
+++ b/solution.py
@@ -27,7 +27,11 @@
 
 def attend_kernel(near, far, first, last, *refs):
     refs = list(refs)
-    lists_ref, q_ref = refs.pop(0), refs.pop(0)
+    lists_hbm = refs.pop(0)
+    if first:
+        q_hbm = refs.pop(0)
+    else:
+        q_high, q_low = refs.pop(0), refs.pop(0)
     near_refs = [[refs.pop(0) for _ in range(pieces)] for _, pieces in near]
     near = [offset for offset, _ in near]
     far_refs = [[refs.pop(0) for _ in range(pieces)] for _, pieces in far]
@@ -38,6 +42,11 @@
         out_hbm = refs.pop(0)
     else:
         acc_out, peak_out, total_out = refs.pop(0), refs.pop(0), refs.pop(0)
+    if first:
+        q_high, q_low = refs.pop(0), refs.pop(0)
+    lists_ref, lists_sem = refs.pop(0), refs.pop(0)
+    if first:
+        q_ref, q_sems = refs.pop(0), refs.pop(0)
     scores = (refs.pop(0), refs.pop(0))
     weights = (refs.pop(0), refs.pop(0))
     fades = (refs.pop(0), refs.pop(0))
@@ -49,15 +58,37 @@
     if last:
         acc_out, out_sem = refs.pop(0), refs.pop(0)
 
-    tokens = q_ref.shape[0]
+    tokens = q_high.shape[0]
     blocks = tokens // BLOCK_TOKENS
     groups = KEY_VALUE_HEADS
     steps = blocks * groups
+
+    def place(step, half):
+        block, group = step // groups, step % groups
+        row = block * BLOCK_TOKENS
+        chain = group * 2 + half
+        col = chain * CHAIN_COLS
+        stat = (block * QUERY_HEADS + chain * CHAIN_HEADS) * BLOCK_TOKENS
+        return block, group, row, col, stat
+
+    read_lists = pltpu.make_async_copy(lists_hbm, lists_ref, lists_sem)
+    read_lists.start()
+
+    def read(step, half):
+        _, _, row, col, _ = place(step, half)
+        at = (pl.ds(row, BLOCK_TOKENS), pl.ds(col, CHAIN_COLS))
+        return pltpu.make_async_copy(q_hbm.at[at], q_ref.at[at], q_sems.at[2 * step + half])
+
     slots = lists_ref.shape[1]
     device = lax.axis_index("ctxhi") * lax.axis_size("ctxlo") + lax.axis_index("ctxlo")
     near_keys = len(near) * tokens
     keys = near_keys + len(far) * BLOCK_TOKENS
     single = keys == BLOCK_TOKENS
+
+    if first:
+        for step in range(steps):
+            for half in range(2):
+                read(step, half).start()
 
     def prepare(pieces, g, k_terms, v_terms, index, at):
         rows = pieces[0].shape[0]
@@ -84,24 +115,18 @@
                 block = [ref.at[b * BLOCK_TOKENS : (b + 1) * BLOCK_TOKENS] for ref in pieces]
                 prepare(block, g, k_far, v_far, b * groups + g, n * BLOCK_TOKENS)
 
-    def place(step, half):
-        block, group = step // groups, step % groups
-        row = pl.multiple_of(block * BLOCK_TOKENS, BLOCK_TOKENS)
-        chain = group * 2 + half
-        col = pl.multiple_of(chain * CHAIN_COLS, HEAD_FEATURES)
-        stat = pl.multiple_of((block * QUERY_HEADS + chain * CHAIN_HEADS) * BLOCK_TOKENS, BLOCK_TOKENS)
-        return block, group, row, col, stat
-
     def score(step, half):
         _, group, row, col, _ = place(step, half)
-        q = jnp.concatenate(
-            [
-                q_ref[pl.ds(row, BLOCK_TOKENS), pl.ds(col + h * HEAD_FEATURES, HEAD_FEATURES)]
-                for h in range(CHAIN_HEADS)
-            ],
-            axis=0,
-        )
-        high, low = split(q * SCALE)
+
+        def cut(h):
+            return pl.ds(row, BLOCK_TOKENS), pl.ds(col + h * HEAD_FEATURES, HEAD_FEATURES)
+
+        if first:
+            read(step, half).wait()
+            for h in range(CHAIN_HEADS):
+                q_high[cut(h)], q_low[cut(h)] = split(q_ref[cut(h)] * SCALE)
+        high = jnp.concatenate([q_high[cut(h)] for h in range(CHAIN_HEADS)], axis=0)
+        low = jnp.concatenate([q_low[cut(h)] for h in range(CHAIN_HEADS)], axis=0)
         dims = (((1,), (1,)), ((), ()))
         if single:
             terms = jnp.concatenate([high, low], axis=1)
@@ -201,6 +226,7 @@
         return pltpu.make_async_copy(acc_out.at[at], out_hbm.at[at], out_sem.at[step])
 
     score(0, 0)
+    read_lists.wait()
     for step in range(steps):
         score(step, 1)
         soften(step, 0)
@@ -220,18 +246,24 @@
 
 
 def attend(lists, query, near, far, carry, last):
-    tokens, width = query.shape
+    tokens, width = query[0].shape
     blocks = tokens // BLOCK_TOKENS
     steps = blocks * KEY_VALUE_HEADS
     first = carry is None
     vmem = pl.BlockSpec(memory_space=pltpu.VMEM)
-    operands = [lists, query, *sum((*near.values(), *far.values()), ())] + ([] if first else list(carry))
-    specs = [pl.BlockSpec(memory_space=pltpu.SMEM)] + [vmem] * (len(operands) - 1)
+    hbm = pl.BlockSpec(memory_space=pltpu.HBM)
+    operands = [lists, *query, *sum((*near.values(), *far.values()), ())]
+    operands += [] if first else list(carry)
+    specs = [hbm] + [hbm if first else vmem] * len(query)
+    specs += [vmem] * (len(operands) - len(specs))
     wide = jax.ShapeDtypeStruct((tokens, width), F32)
     stat = pltpu.VMEM((tokens * QUERY_HEADS, BLOCK_TOKENS), F32)
     near_keys, far_keys = len(near) * tokens, len(far) * BLOCK_TOKENS
     keys = near_keys + far_keys
-    scratch = [pltpu.VMEM((CHAIN_ROWS, keys), F32)] * 2
+    scratch = [pltpu.SMEM(lists.shape, lists.dtype), pltpu.SemaphoreType.DMA]
+    if first:
+        scratch += [pltpu.VMEM((tokens, width), F32), pltpu.SemaphoreType.DMA((2 * steps,))]
+    scratch += [pltpu.VMEM((CHAIN_ROWS, keys), F32)] * 2
     single = keys == BLOCK_TOKENS
     shape = (CHAIN_ROWS, 2 * keys) if single else (2 * CHAIN_ROWS, keys)
     scratch += [pltpu.VMEM(shape, BF16)] * 2
@@ -246,6 +278,8 @@
         out_shape, out_specs = wide, pl.BlockSpec(memory_space=pl.ANY)
     else:
         out_shape, out_specs = (pltpu.VMEM((tokens, width), F32), stat, stat), (vmem,) * 3
+        if first:
+            out_shape, out_specs = out_shape + (pltpu.VMEM((tokens, width), BF16),) * 2, (vmem,) * 5
     pairs = tokens * QUERY_HEADS * keys
 
     def pieces(shards):
@@ -308,7 +342,9 @@
     def shifted(block, offset):
         return move(block, [(i, i + offset) for i in range(devices - offset)])
 
-    own = pack(key_matrix, value_matrix)
+    own = pack(
+        *(pltpu.with_memory_space_constraint(x, pltpu.HBM) for x in (key_matrix, value_matrix))
+    )
     far_offsets = sorted(
         {2**j // blocks for j in range(2, 40) if 2**j < devices * blocks and 2**j // blocks > 2}
     )
@@ -343,10 +379,14 @@
     if turns:
         shards[2] += (move(far[pair][0], turns),)
 
-    def phase(near_offsets, far_offsets, carry, last):
+    lists, query = (
+        pltpu.with_memory_space_constraint(x, pltpu.HBM) for x in (block_lists, query_matrix)
+    )
+
+    def phase(near_offsets, far_offsets, carry, last, query=(query,)):
         return attend(
-            block_lists,
-            query_matrix,
+            lists,
+            query,
             {o: shards[o] for o in near_offsets},
             {o: far[o] for o in far_offsets},
             carry,
@@ -355,12 +395,13 @@
 
     soon = [o for o in (inner, pair) if o in far]
     rest = [o for o in far if o not in soon]
-    carry = phase([0], [], None, False)
-    carry = phase([1], [], carry, False)
-    carry = phase([], soon, carry, False)
-    carry = phase([2], [], carry, not rest)
+    *carry, high, low = phase([0], [], None, False)
+    query = (high, low)
+    carry = phase([1], [], carry, False, query)
+    carry = phase([], soon, carry, False, query)
+    carry = phase([2], [], carry, not rest, query)
     if rest:
-        carry = phase([], rest, carry, True)
+        carry = phase([], rest, carry, True, query)
     return carry if isinstance(carry, jax.Array) else carry[0]
 
 

time: 47.9 us -> 45.4 us (0.948)
  local copies, waits for them, and re-layouts: 3.98 us -> 0 us
  Pallas kernels: 16.2 us -> 17.7 us
    unnamed x10 -> x0, local copies, waits for them, and re-layouts: 3.98 us -> none
    pallas_call x1, Pallas kernels: 0.06 us -> 1.04 us  [pack(): pl.pallas_call(pack_kernel, in_specs=[hbm, hbm], out_specs=pl.BlockSpec(m...]
    pallas_call x5, Pallas kernels: 16.2 us -> 16.7 us  [attend(): pl.pallas_call(functools.partial(attend_kernel, pieces(near), pieces(far)...]
  transfers between devices with their start and end apart: 8 -> 8, of which waited for: 1 -> 1; matrix products, arithmetic and copies ran while one was open for 0% -> 0% of each run, Pallas kernels for 27% -> 30%
where the time goes in v5:
time: 45.4 us; the launch traced here: 45.1 us
  starting transfers between devices  25.6 us (56%)
  Pallas kernels  17.7 us (39%)
  waiting for transfers between devices  1.62 us (4%)
    ppermute x8, starting transfers between devices, move(): lax.ppermute(block, ('ctxlo', 'ctxhi'), [(place(a), place(b)) for a, b in...  25.6 us
    pallas_call x5, Pallas kernels, attend(): pl.pallas_call(functools.partial(attend_kernel, pieces(near), pieces(far)...  16.7 us
    ppermute x8, waiting for transfers between devices, move(): lax.ppermute(block, ('ctxlo', 'ctxhi'), [(place(a), place(b)) for a, b in...  1.62 us
    pallas_call x1, Pallas kernels, pack(): pl.pallas_call(pack_kernel, in_specs=[hbm, hbm], out_specs=pl.BlockSpec(m...  1.04 us
  transfers between devices with their start and end apart: 8, of which 1 were waited for; matrix products, arithmetic and copies ran while one was open for 0% of the time, Pallas kernels for 30%

profile of v5, /device:TPU:0, one launch (start us, length us, event | category | flops | bytes accessed | tf_op | source)
XLA Modules:
  0.0 45.1 jit_solution(11622154023043401445)
XLA Ops:
  0.0 1.0 %pack.1.refs_2_ = f32[256,512]{1,0:T(8,128)S(1)} custom-call(f32[256,256]{1,0:T(8,128)} %k_ref.1, f32[256,256]{1,0:T(8,128)} %v_ref.1), custom_call_target="tpu_custom_call" | custom-call | tf_op jit(solution)/shard_map/pack/pallas_call | solution.py:319
  1.1 0.7 %collective-permute-start.3 = (f32[256,512]{1,0:T(8,128)S(1)}, f32[256,512]{1,0:T(8,128)S(1)}, u32[]{:S(2)}, u32[]{:S(2)}) collective-permute-start(f32[256,512]{1,0:T(8,128)S(1)} %pack.1.refs_2_), channel_id=1, source_target_pairs={{1,3},{9,11},{17,19},{25,27},{3,5},{11,13},{19,21},{27,29},{5,7},{... | collective-permute-start | bytes 1572872 | tf_op jit(solution)/shard_map/ppermute | solution.py:340
  1.8 5.0 %collective-permute-start.1 = (f32[256,512]{1,0:T(8,128)S(1)}, f32[256,512]{1,0:T(8,128)S(1)}, u32[]{:S(2)}, u32[]{:S(2)}) collective-permute-start(f32[256,512]{1,0:T(8,128)S(1)} %pack.1.refs_2_), channel_id=1, source_target_pairs={{0,8},{8,16},{16,24},{24,1},{1,9},{9,17},{17,25},{25,2},{2,10},{10... | collective-permute-start | bytes 1572872 | tf_op jit(solution)/shard_map/ppermute | solution.py:340
  6.8 3.9 %collective-permute-start.5 = (f32[256,512]{1,0:T(8,128)S(1)}, f32[256,512]{1,0:T(8,128)S(1)}, u32[]{:S(2)}, u32[]{:S(2)}) collective-permute-start(f32[256,512]{1,0:T(8,128)S(1)} %pack.1.refs_2_), channel_id=1, source_target_pairs={{0,1},{8,9},{16,17},{24,25},{2,3},{10,11},{18,19},{26,27},{4,5},{1... | collective-permute-start | bytes 1572872 | tf_op jit(solution)/shard_map/ppermute | solution.py:340
  10.7 3.4 %collective-permute-start.7 = (f32[256,512]{1,0:T(8,128)S(1)}, f32[256,512]{1,0:T(8,128)S(1)}, u32[]{:S(2)}, u32[]{:S(2)}) collective-permute-start(f32[256,512]{1,0:T(8,128)S(1)} %pack.1.refs_2_), channel_id=1, source_target_pairs={{0,2},{8,10},{16,18},{24,26},{2,4},{10,12},{18,20},{26,28},{4,6},{... | collective-permute-start | bytes 1572872 | tf_op jit(solution)/shard_map/ppermute | solution.py:340
  14.1 0.0 collective-permute-done.3.refs_5_
  14.1 1.3 %collective-permute-start.6 = (f32[256,512]{1,0:T(8,128)S(1)}, f32[256,512]{1,0:T(8,128)S(1)}, u32[]{:S(2)}, u32[]{:S(2)}) collective-permute-start(f32[256,512]{1,0:T(8,128)S(1)} %collective-permute-done.3.refs_5_), channel_id=1, source_target_pairs={{1,0},{9,8},{17,16},{25,24},{3,2},{11,10},{19,18},{27,26},{5,4},{1... | collective-permute-start | bytes 1572872 | tf_op jit(solution)/shard_map/ppermute | solution.py:340
  15.4 0.7 %collective-permute-start.4 = (f32[256,512]{1,0:T(8,128)S(1)}, f32[256,512]{1,0:T(8,128)S(1)}, u32[]{:S(2)}, u32[]{:S(2)}) collective-permute-start(f32[256,512]{1,0:T(8,128)S(1)} %collective-permute-done.3.refs_5_), channel_id=1, source_target_pairs={{19,2},{21,4},{23,6}} | collective-permute-start | bytes 1572872 | tf_op jit(solution)/shard_map/ppermute | solution.py:340
  16.1 1.6 %collective-permute-done.1.refs_3_ = f32[256,512]{1,0:T(8,128)S(1)} collective-permute-done((f32[256,512]{1,0:T(8,128)S(1)}, f32[256,512]{1,0:T(8,128)S(1)}, u32[]{:S(2)}, u32[]{:S(2)}) %collective-permute-start.1) | collective-permute-done | bytes 524320 | tf_op jit(solution)/shard_map/ppermute | solution.py:340
  17.7 4.4 %collective-permute-start.2 = (f32[256,512]{1,0:T(8,128)S(1)}, f32[256,512]{1,0:T(8,128)S(1)}, u32[]{:S(2)}, u32[]{:S(2)}) collective-permute-start(f32[256,512]{1,0:T(8,128)S(1)} %collective-permute-done.1.refs_3_), channel_id=1, source_target_pairs={{0,8},{8,16},{16,24},{24,1},{1,9},{9,17},{17,25},{2,10},{10,18},{1... | collective-permute-start | bytes 1572872 | tf_op jit(solution)/shard_map/ppermute | solution.py:340
  22.1 0.0 collective-permute-done.5.refs_3_
  22.1 6.2 %collective-permute-start = (f32[256,512]{1,0:T(8,128)S(1)}, f32[256,512]{1,0:T(8,128)S(1)}, u32[]{:S(2)}, u32[]{:S(2)}) collective-permute-start(f32[256,512]{1,0:T(8,128)S(1)} %pack.1.refs_2_), channel_id=1, source_target_pairs={{0,4},{8,12},{16,20},{24,28},{1,5},{9,13},{17,21},{25,29},{2,6},{1... | collective-permute-start | bytes 1572872 | tf_op jit(solution)/shard_map/ppermute | solution.py:340
  28.3 4.5 %shard_map.46 = (f32[256,1536]{1,0:T(8,128)S(1)}, f32[3072,128]{1,0:T(8,128)S(1)}, f32[3072,128]{1,0:T(8,128)S(1)}, bf16[256,1536]{1,0:T(8,128)(2,1)S(1)}, bf16[256,1536]{1,0:T(8,128)(2,1)S(1)}) custom-call(s32[2,15]{1,0:T(2,128)} %refs_0_.9, f32[256,1536]{1,0:T(8,128)} %refs_1_.1, f32[256,512]{1,0:T(8,128)S(1)} %pack.1.refs_2_), custom_call_target="tpu_custom_call" | custom-call | flops 1610612736 | bytes 6291456 | tf_op jit(solution)/shard_map/pallas_call | solution.py:288
  32.8 3.0 %shard_map.47 = (f32[256,1536]{1,0:T(8,128)S(1)}, f32[3072,128]{1,0:T(8,128)S(1)}, f32[3072,128]{1,0:T(8,128)S(1)}) custom-call(s32[2,15]{1,0:T(2,128)} %refs_0_.9, bf16[256,1536]{1,0:T(8,128)(2,1)S(1)} %get-tuple-element.19.refs_1_, bf16[256,1536]{1,0:T(8,128)(2,1)S(1)} %get-tuple-element.20.refs_2_, f32[256,512]{1,0:T(8,128)S(1)} %collective-permute-done.1.refs_3_, ...), custom_call_target="tpu_custom_call" | custom-call | flops 1610612736 | bytes 6291456 | tf_op jit(solution)/shard_map/pallas_call | solution.py:288
  35.8 0.0 collective-permute-done.7.refs_6_
  35.8 0.0 collective-permute-done.6.refs_4_
  35.9 3.0 %shard_map.48 = (f32[256,1536]{1,0:T(8,128)S(1)}, f32[3072,128]{1,0:T(8,128)S(1)}, f32[3072,128]{1,0:T(8,128)S(1)}) custom-call(s32[2,15]{1,0:T(2,128)} %refs_0_.9, bf16[256,1536]{1,0:T(8,128)(2,1)S(1)} %get-tuple-element.19.refs_1_, bf16[256,1536]{1,0:T(8,128)(2,1)S(1)} %get-tuple-element.20.refs_2_, f32[256,512]{1,0:T(8,128)S(1)} %collective-permute-done.5.refs_3_, ...), custom_call_target="tpu_custom_call" | custom-call | flops 1610612736 | bytes 6291456 | tf_op jit(solution)/shard_map/pallas_call | solution.py:288
  38.9 0.0 collective-permute-done.4.refs_4_
  38.9 0.0 collective-permute-done.2.refs_3_
  38.9 3.0 %shard_map.49 = (f32[256,1536]{1,0:T(8,128)S(1)}, f32[3072,128]{1,0:T(8,128)S(1)}, f32[3072,128]{1,0:T(8,128)S(1)}) custom-call(s32[2,15]{1,0:T(2,128)} %refs_0_.9, bf16[256,1536]{1,0:T(8,128)(2,1)S(1)} %get-tuple-element.19.refs_1_, bf16[256,1536]{1,0:T(8,128)(2,1)S(1)} %get-tuple-element.20.refs_2_, f32[256,512]{1,0:T(8,128)S(1)} %collective-permute-done.2.refs_3_, ...), custom_call_target="tpu_custom_call" | custom-call | flops 1610612736 | bytes 6291456 | tf_op jit(solution)/shard_map/pallas_call | solution.py:288
  41.9 0.0 collective-permute-done.refs_3_
  41.9 3.2 %shard_map.50 = f32[256,1536]{1,0:T(8,128)} custom-call(s32[2,15]{1,0:T(2,128)} %refs_0_.9, bf16[256,1536]{1,0:T(8,128)(2,1)S(1)} %get-tuple-element.19.refs_1_, bf16[256,1536]{1,0:T(8,128)(2,1)S(1)} %get-tuple-element.20.refs_2_, f32[256,512]{1,0:T(8,128)S(1)} %collective-permute-done.refs_3_, f32[256,1536]{1,0:T(8,128)S(1)} %get-tuple-element.30.refs_4_, ...), custom_call_target="tpu_custom_call" | custom-call | flops 805306368 | bytes 6291456 | tf_op jit(solution)/shard_map/pallas_call | solution.py:288
Async XLA Ops:
  1.1 13.0 %collective-permute-start.3 = (f32[256,512]{1,0:T(8,128)S(1)}, f32[256,512]{1,0:T(8,128)S(1)}, u32[]{:S(2)}, u32[]{:S(2)}) collective-permute-start(f32[256,512]{1,0:T(8,128)S(1)} %pack.1.refs_2_), channel_id=1, source_target_pairs={{1,3},{9,11},{17,19},{25,27},{3,5},{11,13},{19,21},{27,29},{5,7},{... | collective-permute-start | bytes 1572872 | tf_op jit(solution)/shard_map/ppermute | solution.py:340
  1.8 15.9 %collective-permute-start.1 = (f32[256,512]{1,0:T(8,128)S(1)}, f32[256,512]{1,0:T(8,128)S(1)}, u32[]{:S(2)}, u32[]{:S(2)}) collective-permute-start(f32[256,512]{1,0:T(8,128)S(1)} %pack.1.refs_2_), channel_id=1, source_target_pairs={{0,8},{8,16},{16,24},{24,1},{1,9},{9,17},{17,25},{25,2},{2,10},{10... | collective-permute-start | bytes 1572872 | tf_op jit(solution)/shard_map/ppermute | solution.py:340
  6.8 15.4 %collective-permute-start.5 = (f32[256,512]{1,0:T(8,128)S(1)}, f32[256,512]{1,0:T(8,128)S(1)}, u32[]{:S(2)}, u32[]{:S(2)}) collective-permute-start(f32[256,512]{1,0:T(8,128)S(1)} %pack.1.refs_2_), channel_id=1, source_target_pairs={{0,1},{8,9},{16,17},{24,25},{2,3},{10,11},{18,19},{26,27},{4,5},{1... | collective-permute-start | bytes 1572872 | tf_op jit(solution)/shard_map/ppermute | solution.py:340
  10.7 25.2 %collective-permute-start.7 = (f32[256,512]{1,0:T(8,128)S(1)}, f32[256,512]{1,0:T(8,128)S(1)}, u32[]{:S(2)}, u32[]{:S(2)}) collective-permute-start(f32[256,512]{1,0:T(8,128)S(1)} %pack.1.refs_2_), channel_id=1, source_target_pairs={{0,2},{8,10},{16,18},{24,26},{2,4},{10,12},{18,20},{26,28},{4,6},{... | collective-permute-start | bytes 1572872 | tf_op jit(solution)/shard_map/ppermute | solution.py:340
  14.1 21.8 %collective-permute-start.6 = (f32[256,512]{1,0:T(8,128)S(1)}, f32[256,512]{1,0:T(8,128)S(1)}, u32[]{:S(2)}, u32[]{:S(2)}) collective-permute-start(f32[256,512]{1,0:T(8,128)S(1)} %collective-permute-done.3.refs_5_), channel_id=1, source_target_pairs={{1,0},{9,8},{17,16},{25,24},{3,2},{11,10},{19,18},{27,26},{5,4},{1... | collective-permute-start | bytes 1572872 | tf_op jit(solution)/shard_map/ppermute | solution.py:340
  15.4 23.5 %collective-permute-start.4 = (f32[256,512]{1,0:T(8,128)S(1)}, f32[256,512]{1,0:T(8,128)S(1)}, u32[]{:S(2)}, u32[]{:S(2)}) collective-permute-start(f32[256,512]{1,0:T(8,128)S(1)} %collective-permute-done.3.refs_5_), channel_id=1, source_target_pairs={{19,2},{21,4},{23,6}} | collective-permute-start | bytes 1572872 | tf_op jit(solution)/shard_map/ppermute | solution.py:340
  17.7 21.2 %collective-permute-start.2 = (f32[256,512]{1,0:T(8,128)S(1)}, f32[256,512]{1,0:T(8,128)S(1)}, u32[]{:S(2)}, u32[]{:S(2)}) collective-permute-start(f32[256,512]{1,0:T(8,128)S(1)} %collective-permute-done.1.refs_3_), channel_id=1, source_target_pairs={{0,8},{8,16},{16,24},{24,1},{1,9},{9,17},{17,25},{2,10},{10,18},{1... | collective-permute-start | bytes 1572872 | tf_op jit(solution)/shard_map/ppermute | solution.py:340
  22.1 19.8 %collective-permute-start = (f32[256,512]{1,0:T(8,128)S(1)}, f32[256,512]{1,0:T(8,128)S(1)}, u32[]{:S(2)}, u32[]{:S(2)}) collective-permute-start(f32[256,512]{1,0:T(8,128)S(1)} %pack.1.refs_2_), channel_id=1, source_target_pairs={{0,4},{8,12},{16,20},{24,28},{1,5},{9,13},{17,21},{25,29},{2,6},{1... | collective-permute-start | bytes 1572872 | tf_op jit(solution)/shard_map/ppermute | solution.py:340
